TPU v7x, 128 devices: a whole 4x4x4 slice. The times are simulated.
128 devices in a mesh: row: 16 (over y_hi, x, core), col: 8 (over z, y_lo).
Axes of the slice: x: 4, y: 4 (y_hi: 2, y_lo: 2; y = y_hi * 2 + y_lo), z: 4, core: 2. Of those that a mesh axis runs over, the one named last changes fastest.
Arguments:
- orbitals_in: float32 [16384, 256], P(('row', 'col')), may hold values from -6 to 6
- hblocks: bfloat16 [256, 128, 4096], P('row', 'col'), may hold values from -0.046875 to 0.046875
- block_cols: int32 [256, 128], P('row', 'col'), may hold values from 0 to 31, as said below
- live_counts: int32 [256, 8], P('row', 'col'), may hold values from 0 to 16, as said below
- onsite: bfloat16 [256, 4096], P(('row', 'col')), may hold values from -3 to 1, as said below
- cut_low: float32 [1], replicated, may hold values from -1.6 to -1
- top_bound: float32 [1], replicated, may hold values from 2.4 to 3.2
Outputs:
- orbitals: float32 [16384, 256], P(('row', 'col'))
- projected: float32 [256, 256], replicated
Inputs may be any that keep to these rules, and one draw needn't show every extreme that they name: `block_cols`: in block row b and column group c the first live_counts[b, c] slots name distinct block columns whose global block index exceeds b (strict upper triangle); the other slots are padding and are ignored. `live_counts`: block row 0 fills all 16 slots of every column group; the last block row has no live slot. `onsite`: every block is symmetric.
All inputs are finite; a program needn't handle non-finite values.
Results may differ from a plain program's by a relative error of at most 0.0008.
The roundings to bfloat16 on the way count: a program that leaves them out, or rounds other values in their place, can miss the bound.
Values may be sent and summed in bfloat16 or wider, within the bound.
A program may use at most 128 MiB of HBM per device.

v0:
```python
import jax
import jax.numpy as jnp
from jax import lax
from jax.sharding import PartitionSpec as P

BS = 64
K = 256
PB = 2
DEG = 3


def add_columns(dense_tile, portion):
    return jnp.dot(dense_tile, portion, preferred_element_type=jnp.float32)


def mirror_rows(dense_tile, row_set):
    return lax.dot_general(
        dense_tile, row_set, (((0,), (0,)), ((), ())), preferred_element_type=jnp.float32
    )


def build_tile(hblocks, block_cols, live_counts, column_blocks):
    row_blocks, slot_count, _ = hblocks.shape
    occupied = jnp.arange(slot_count, dtype=jnp.int32)[None, :] < live_counts
    selector = (
        block_cols[:, :, None] == jnp.arange(column_blocks, dtype=jnp.int32)[None, None, :]
    ) & occupied[:, :, None]
    blocks = hblocks.reshape(row_blocks, slot_count, BS, BS)
    dense_tile = jnp.einsum(
        "isc,isab->iacb", selector.astype(jnp.bfloat16), blocks, preferred_element_type=jnp.float32
    )
    return dense_tile.astype(jnp.bfloat16).reshape(row_blocks * BS, column_blocks * BS)


def local(orbitals_in, hblocks, block_cols, live_counts, onsite, cut_low, top_bound):
    row_devices = lax.axis_size("row")
    col_devices = lax.axis_size("col")
    column_blocks = row_devices * PB
    local_rows = PB * BS
    total_rows = row_devices * col_devices * local_rows
    dense_tile = build_tile(hblocks, block_cols, live_counts, column_blocks)
    onsite_blocks = onsite.reshape(PB, BS, BS)

    def reduce_direct(terms):
        return lax.psum_scatter(terms, "col", scatter_dimension=0, tiled=True)

    def apply(rounded):
        onsite_part = jnp.einsum(
            "pab,pbk->pak",
            onsite_blocks,
            rounded.reshape(PB, BS, K),
            preferred_element_type=jnp.float32,
        ).reshape(local_rows, K)
        direct = reduce_direct(
            add_columns(dense_tile, lax.all_gather(rounded, "row", axis=0, tiled=True))
        )
        mirror = lax.psum_scatter(
            mirror_rows(dense_tile, lax.all_gather(rounded, "col", axis=0, tiled=True)),
            "row",
            scatter_dimension=0,
            tiled=True,
        )
        return onsite_part + direct + mirror

    centre = 0.5 * (top_bound[0] + cut_low[0])
    halfwidth = 0.5 * (top_bound[0] - cut_low[0])
    previous = orbitals_in
    current = (apply(orbitals_in.astype(jnp.bfloat16)) - centre * orbitals_in) / halfwidth
    for degree in range(DEG - 1):
        following = (
            2.0 * (apply(current.astype(jnp.bfloat16)) - centre * current) / halfwidth - previous
        )
        previous, current = (current, following)
    rounded = current.astype(jnp.bfloat16)
    as_float = rounded.astype(jnp.float32)
    contract = (((0,), (0,)), ((), ()))
    gram_part = lax.dot_general(rounded, rounded, contract, preferred_element_type=jnp.float32)
    image = apply(rounded)
    cross_part = lax.dot_general(as_float, image, contract, precision=lax.Precision.HIGHEST)
    gram_total, cross_total = lax.psum((gram_part, cross_part), ("row", "col"))
    gram_matrix = gram_total / total_rows
    ritz_matrix = (cross_total + cross_total.T) / (2.0 * total_rows)
    factor = jnp.linalg.cholesky(gram_matrix)
    orbitals = jax.scipy.linalg.solve_triangular(factor, current.T, lower=True).T
    inner = jax.scipy.linalg.solve_triangular(factor, ritz_matrix, lower=True)
    projected = jax.scipy.linalg.solve_triangular(factor, inner.T, lower=True)
    return (orbitals, projected)


def solution(mesh):
    placed = (
        P(("row", "col"), None),
        P("row", "col", None),
        P("row", "col"),
        P("row", "col"),
        P(("row", "col"), None),
        P(),
        P(),
    )
    return jax.shard_map(
        local, mesh=mesh, in_specs=placed, out_specs=(P(("row", "col"), None), P()), check_vma=False
    )
```

profile of v0, /device:TPU:1, one launch (start us, length us, event | category | flops | bytes accessed | tf_op | source)
XLA Modules:
  0.0 903.4 jit_solution(17615895773485688638)
XLA Ops:
  8.8 6.9 reshape.92
  15.8 8.9 convert_bitcast_fusion
  24.7 12.4 %reshape.93 = bf16[1024,2048]{1,0:T(8,128)(2,1)} reshape(bf16[16,64,32,64]{3,2,1,0:T(8,128)(2,1)} %convert_bitcast_fusion) | data formatting | bytes 8388608 | tf_op jit(solution)/shard_map/reshape | solution.py:32
  37.1 29.5 %all_gather.25 = bf16[1024,256]{1,0:T(8,128)(2,1)S(1)} all-gather(bf16[128,256]{1,0:T(8,128)(2,1)S(1)} %copy-done.2), channel_id=1, replica_groups=mesh['row'=16,'col'=8] {'col'}, dimensions={0}, use_global_device_ids=true | all-gather | bytes 589824 | tf_op jit(solution)/shard_map/all_gather | solution.py:58
  77.9 67.4 %reduce-scatter.11.cloned.1.call-done = f32[128,256]{1,0:T(8,128)} async-done(((f32[2048,256]{1,0:T(8,128)}), f32[128,256]{1,0:T(8,128)}) %reduce-scatter.11.cloned.1.call-update) | async-done | bytes 131088 | tf_op jit(solution)/shard_map/reduce_scatter | solution.py:57
  145.3 39.7 %reduce-scatter.9.cloned.1.call-done = f32[128,256]{1,0:T(8,128)} async-done(((f32[1024,256]{1,0:T(8,128)}), f32[128,256]{1,0:T(8,128)}) %reduce-scatter.9.cloned.1.call-update) | async-done | bytes 131088 | tf_op jit(solution)/shard_map/reduce_scatter | solution.py:45
  186.7 23.9 %all_gather.27 = bf16[1024,256]{1,0:T(8,128)(2,1)S(1)} all-gather(bf16[128,256]{1,0:T(8,128)(2,1)} %get-tuple-element.43), channel_id=1, replica_groups=mesh['row'=16,'col'=8] {'col'}, dimensions={0}, use_global_device_ids=true | all-gather | bytes 589824 | tf_op jit(solution)/shard_map/all_gather | solution.py:58
  215.6 21.6 %all-gather.7.cloned.1.call-done = bf16[2048,256]{1,0:T(8,128)(2,1)} async-done(((bf16[128,256]{1,0:T(8,128)(2,1)}), bf16[2048,256]{1,0:T(8,128)(2,1)}) %all-gather.7.cloned.1.call-update) | async-done | bytes 1048592 | tf_op jit(solution)/shard_map/all_gather | solution.py:55
  242.1 66.2 %reduce-scatter.15.cloned.1.call-done = f32[128,256]{1,0:T(8,128)} async-done(((f32[2048,256]{1,0:T(8,128)}), f32[128,256]{1,0:T(8,128)}) %reduce-scatter.15.cloned.1.call-update) | async-done | bytes 131088 | tf_op jit(solution)/shard_map/reduce_scatter | solution.py:57
  308.3 39.6 %reduce-scatter.13.cloned.1.call-done = f32[128,256]{1,0:T(8,128)} async-done(((f32[1024,256]{1,0:T(8,128)}), f32[128,256]{1,0:T(8,128)}) %reduce-scatter.13.cloned.1.call-update) | async-done | bytes 131088 | tf_op jit(solution)/shard_map/reduce_scatter | solution.py:45
  349.7 24.2 %all_gather.29 = bf16[1024,256]{1,0:T(8,128)(2,1)S(1)} all-gather(bf16[128,256]{1,0:T(8,128)(2,1)} %get-tuple-element.41), channel_id=1, replica_groups=mesh['row'=16,'col'=8] {'col'}, dimensions={0}, use_global_device_ids=true | all-gather | bytes 589824 | tf_op jit(solution)/shard_map/all_gather | solution.py:58
  373.9 4.8 fusion.50
  378.8 21.2 %all-gather.9.cloned.1.call-done = bf16[2048,256]{1,0:T(8,128)(2,1)} async-done(((bf16[128,256]{1,0:T(8,128)(2,1)}), bf16[2048,256]{1,0:T(8,128)(2,1)}) %all-gather.9.cloned.1.call-update) | async-done | bytes 1048592 | tf_op jit(solution)/shard_map/all_gather | solution.py:55
  405.0 66.3 %reduce-scatter.19.cloned.1.call-done = f32[128,256]{1,0:T(8,128)} async-done(((f32[2048,256]{1,0:T(8,128)}), f32[128,256]{1,0:T(8,128)}) %reduce-scatter.19.cloned.1.call-update) | async-done | bytes 131088 | tf_op jit(solution)/shard_map/reduce_scatter | solution.py:57
  471.3 39.7 %reduce-scatter.17.cloned.1.call-done = f32[128,256]{1,0:T(8,128)} async-done(((f32[1024,256]{1,0:T(8,128)}), f32[128,256]{1,0:T(8,128)}) %reduce-scatter.17.cloned.1.call-update) | async-done | bytes 131088 | tf_op jit(solution)/shard_map/reduce_scatter | solution.py:45
  512.8 24.1 %all_gather.31 = bf16[1024,256]{1,0:T(8,128)(2,1)S(1)} all-gather(bf16[128,256]{1,0:T(8,128)(2,1)} %get-tuple-element.39), channel_id=1, replica_groups=mesh['row'=16,'col'=8] {'col'}, dimensions={0}, use_global_device_ids=true | all-gather | bytes 589824 | tf_op jit(solution)/shard_map/all_gather | solution.py:58
  541.8 21.2 %all-gather.11.cloned.1.call-done = bf16[2048,256]{1,0:T(8,128)(2,1)} async-done(((bf16[128,256]{1,0:T(8,128)(2,1)}), bf16[2048,256]{1,0:T(8,128)(2,1)}) %all-gather.11.cloned.1.call-update) | async-done | bytes 1048592 | tf_op jit(solution)/shard_map/all_gather | solution.py:55
  568.9 65.4 %reduce-scatter.23.cloned.1.call-done = f32[128,256]{1,0:T(8,128)} async-done(((f32[2048,256]{1,0:T(8,128)}), f32[128,256]{1,0:T(8,128)}) %reduce-scatter.23.cloned.1.call-update) | async-done | bytes 131088 | tf_op jit(solution)/shard_map/reduce_scatter | solution.py:57
  634.3 39.6 %reduce-scatter.21.cloned.1.call-done = f32[128,256]{1,0:T(8,128)} async-done(((f32[1024,256]{1,0:T(8,128)}), f32[128,256]{1,0:T(8,128)}) %reduce-scatter.21.cloned.1.call-update) | async-done | bytes 131088 | tf_op jit(solution)/shard_map/reduce_scatter | solution.py:45
  675.9 152.6 %all-reduce.4.cloned.1.call-done = (f32[256,256]{0,1:T(8,128)}, f32[256,256]{1,0:T(8,128)}) async-done(((f32[256,256]{0,1:T(8,128)}, f32[256,256]{1,0:T(8,128)}), (f32[256,256]{0,1:T(8,128)}, f32[256,256]{1,0:T(8,128)})) %all-reduce.4.cloned.1.call-update) | async-done | bytes 524304 | tf_op jit(solution)/shard_map/psum | solution.py:80
  831.9 11.7 %cholesky.50 = f32[128,128]{1,0:T(8,128)S(1)} custom-call(f32[128,128]{1,0:T(8,128)S(1)} %cholesky.118), custom_call_target="Cholesky" | custom-call | tf_op jit(solution)/shard_map/jit(cholesky)/cholesky | solution.py:83
  843.7 9.8 %custom-call.18 = f32[1,128,128]{1,2,0:T(8,128)S(1)} custom-call(f32[1,128,128]{2,1,0:T(8,128)S(1)} %get-tuple-element.50), custom_call_target="InvertDiagBlocksLowerTriangular" | custom-call | tf_op jit(solution)/shard_map/jit(cholesky)/cholesky | solution.py:83
  854.0 11.7 %cholesky.105 = f32[128,128]{1,0:T(8,128)S(1)} custom-call(f32[128,128]{1,0:T(8,128)S(1)} %convolution_subtract_fusion.3), custom_call_target="Cholesky" | custom-call | tf_op jit(solution)/shard_map/jit(cholesky)/cholesky | solution.py:83
  872.8 19.7 %custom-call.19 = f32[2,128,128]{1,2,0:T(8,128)S(1)} custom-call(f32[2,128,128]{2,1,0:T(8,128)S(1)} %get-tuple-element.18), custom_call_target="InvertDiagBlocksLowerTriangular" | custom-call | tf_op jit(solution)/shard_map/jit(_solve_triangular)/triangular_solve | solution.py:84
  (99 shorter events, 62.2 us)
Async XLA Ops:
  7.2 8.6 copy-start.7
  7.2 8.7 copy-start.6
  7.2 64.4 %all-gather.5.cloned.1.call-start = ((), (), s32[]{:S(2)}) async-start(), calls=%async_computation.8 | async-start | bytes 1114112 | tf_op jit(solution)/shard_map/all_gather | solution.py:55
  8.8 136.5 %reduce-scatter.11.cloned.1.call-start = ((), (), s32[]{:S(2)}) async-start(), calls=%async_computation.10 | async-start | bytes 2228224 | tf_op jit(solution)/shard_map/reduce_scatter | solution.py:57
  24.7 12.4 %copy-start.2 = (bf16[128,256]{1,0:T(8,128)(2,1)S(1)}, bf16[128,256]{1,0:T(8,128)(2,1)}, u32[]{:S(2)}) copy-start(bf16[128,256]{1,0:T(8,128)(2,1)} %convert_element_type.20) | copy-start | bytes 196612
  71.5 6.2 copy-start.5
  71.5 113.6 %copy-start.1 = (f32[128,256]{1,0:T(8,128)S(1)}, f32[128,256]{1,0:T(8,128)}, u32[]{:S(2)}) copy-start(f32[128,256]{1,0:T(8,128)} %param.9) | copy-start | bytes 393220
  71.5 113.6 %reduce-scatter.9.cloned.1.call-start = ((), (), s32[]{:S(2)}) async-start(), calls=%async_computation.9 | async-start | bytes 1179648 | tf_op jit(solution)/shard_map/reduce_scatter | solution.py:45
  76.3 160.9 %all-gather.7.cloned.1.call-start = ((), (), s32[]{:S(2)}) async-start(), calls=%async_computation.11 | async-start | bytes 1114112 | tf_op jit(solution)/shard_map/all_gather | solution.py:55
  186.7 121.6 %reduce-scatter.15.cloned.1.call-start = ((), (), s32[]{:S(2)}) async-start(), calls=%async_computation.13 | async-start | bytes 2228224 | tf_op jit(solution)/shard_map/reduce_scatter | solution.py:57
  215.5 26.5 %copy-start.3 = (bf16[128,256]{1,0:T(8,128)(2,1)S(1)}, bf16[128,256]{1,0:T(8,128)(2,1)}, u32[]{:S(2)}) copy-start(bf16[128,256]{1,0:T(8,128)(2,1)} %get-tuple-element.43) | copy-start | bytes 196612
  215.5 132.4 %reduce-scatter.13.cloned.1.call-start = ((), (), s32[]{:S(2)}) async-start(), calls=%async_computation.12 | async-start | bytes 1179648 | tf_op jit(solution)/shard_map/reduce_scatter | solution.py:45
  241.9 158.1 %all-gather.9.cloned.1.call-start = ((), (), s32[]{:S(2)}) async-start(), calls=%async_computation.14 | async-start | bytes 1114112 | tf_op jit(solution)/shard_map/all_gather | solution.py:55
  349.6 121.7 %reduce-scatter.19.cloned.1.call-start = ((), (), s32[]{:S(2)}) async-start(), calls=%async_computation.16 | async-start | bytes 2228224 | tf_op jit(solution)/shard_map/reduce_scatter | solution.py:57
  378.7 26.1 %copy-start.4 = (bf16[128,256]{1,0:T(8,128)(2,1)S(1)}, bf16[128,256]{1,0:T(8,128)(2,1)}, u32[]{:S(2)}) copy-start(bf16[128,256]{1,0:T(8,128)(2,1)} %get-tuple-element.41) | copy-start | bytes 196612
  378.7 132.3 %reduce-scatter.17.cloned.1.call-start = ((), (), s32[]{:S(2)}) async-start(), calls=%async_computation.15 | async-start | bytes 1179648 | tf_op jit(solution)/shard_map/reduce_scatter | solution.py:45
  404.8 158.2 %all-gather.11.cloned.1.call-start = ((), (), s32[]{:S(2)}) async-start(), calls=%async_computation.17 | async-start | bytes 1114112 | tf_op jit(solution)/shard_map/all_gather | solution.py:55
  512.7 121.6 %reduce-scatter.23.cloned.1.call-start = ((), (), s32[]{:S(2)}) async-start(), calls=%async_computation.19 | async-start | bytes 2228224 | tf_op jit(solution)/shard_map/reduce_scatter | solution.py:57
  541.7 26.1 %copy-start = (bf16[128,256]{1,0:T(8,128)(2,1)S(1)}, bf16[128,256]{1,0:T(8,128)(2,1)}, u32[]{:S(2)}) copy-start(bf16[128,256]{1,0:T(8,128)(2,1)} %get-tuple-element.39) | copy-start | bytes 196612
  541.7 132.2 %reduce-scatter.21.cloned.1.call-start = ((), (), s32[]{:S(2)}) async-start(), calls=%async_computation.18 | async-start | bytes 1179648 | tf_op jit(solution)/shard_map/reduce_scatter | solution.py:45
  567.8 260.8 %all-reduce.4.cloned.1.call-start = ((), (), s32[]{:S(2)}) async-start(), calls=%async_computation.20 | async-start | bytes 1048576 | tf_op jit(solution)/shard_map/psum | solution.py:80
Sparse Core Ops, SparseCore 0:
  11.0 50.9 all-gather.4
  71.6 73.7 reduce-scatter.10
  147.7 37.2 reduce-scatter.8
  187.9 49.2 all-gather.6
  241.0 67.3 reduce-scatter.14
  310.6 37.3 reduce-scatter.12
  351.0 49.0 all-gather.8
  404.0 67.3 reduce-scatter.18
  473.7 37.2 reduce-scatter.16
  513.9 49.0 all-gather.10
  566.9 67.3 reduce-scatter.22
  636.5 37.3 reduce-scatter.20
  679.4 149.1 all-reduce.3
where the time goes:
time: 904 us; the launch traced here: 903 us
  waiting for transfers between devices  641 us (71%)
  blocking collectives  102 us (11%)
  other arithmetic  64.7 us (7%)
  matrix products  52.9 us (6%)
  local copies, waits for them, and re-layouts  25.5 us (3%)
  between operations  16.8 us (2%)
    reduce_scatter x4, waiting for transfers between devices, apply(): lax.psum_scatter(mirror_rows(dense_tile, lax.all_gather(rounded, 'col', a...  265 us
    reduce_scatter x4, waiting for transfers between devices, reduce_direct(): return lax.psum_scatter(terms, 'col', scatter_dimension=0, tiled=True)  159 us
    psum x1, waiting for transfers between devices, local(): gram_total, cross_total = lax.psum((gram_part, cross_part), ('row', 'col'))  153 us
    all_gather x4, blocking collectives, apply(): lax.all_gather(rounded, 'col', axis=0, tiled=True)  102 us
    all_gather x4, waiting for transfers between devices, apply(): lax.all_gather(rounded, 'row', axis=0, tiled=True)  64.1 us
    another operation x7, other arithmetic, local(): factor = jnp.linalg.cholesky(gram_matrix)  34.7 us
    another operation x3, other arithmetic, local(): jax.scipy.linalg.solve_triangular(factor, current.T, lower=True)  19.7 us
    dot_general x4, matrix products, mirror_rows(): lax.dot_general(dense_tile, row_set, (((0,), (0,)), ((), ())), preferred_...  19.4 us
  transfers between devices with their start and end apart: 13, of which 12 were waited for; matrix products, arithmetic and copies ran while one was open for 8% of the time, Pallas kernels for 0%

commit v1 on v0

v1 whole, which is shorter than its diff:
```python
import jax
import jax.numpy as jnp
from jax import lax
from jax.experimental import pallas as pl
from jax.experimental.pallas import tpu as pltpu
from jax.sharding import PartitionSpec as P

BS = 64
K = 256
PB = 2
DEG = 3
LR = PB * BS
MESH = pl.DeviceIdType.MESH
F32 = jnp.float32
BF16 = jnp.bfloat16

NR = 16
NC = 8
SLAB = K // NR


def build_tile(hblocks, block_cols, live_counts, column_blocks):
    row_blocks, slot_count, _ = hblocks.shape
    occupied = jnp.arange(slot_count, dtype=jnp.int32)[None, :] < live_counts
    selector = (
        block_cols[:, :, None] == jnp.arange(column_blocks, dtype=jnp.int32)[None, None, :]
    ) & occupied[:, :, None]
    blocks = hblocks.reshape(row_blocks, slot_count, BS, BS)
    dense_tile = jnp.einsum(
        "isc,isab->iacb", selector.astype(jnp.bfloat16), blocks, preferred_element_type=jnp.float32
    )
    return dense_tile.astype(jnp.bfloat16).reshape(row_blocks * BS, column_blocks * BS)


def rcopy(src, dst, ssem, rsem, dev):
    return pltpu.make_async_remote_copy(
        src_ref=src, dst_ref=dst, send_sem=ssem, recv_sem=rsem, device_id=dev, device_id_type=MESH
    )


def contract_rows(a, b):
    return lax.dot_general(a, b, (((0,), (0,)), ((), ())), preferred_element_type=F32)


def kernel(
    tile, tile_t, y0, onsite, low, top, y_out, gram_out, ritz_out,
    vc, vr, ms, sr, mx, xr, zs, zr, ys, yr, ls, lr, prev, cur, part, a1, s2, a2,
    ag_s, ag_r, rs_s, rs_r, ar_s, ar_r,
):
    r = lax.axis_index("row")
    c = lax.axis_index("col")
    core = lax.rem(r, 2)
    x = lax.rem(r // 2, 4)
    yh = r // 8
    z = c // 2
    yl = lax.rem(c, 2)
    sib_r = r + 1 - 2 * core
    yhp_r = lax.rem(r + 8, NR)
    ylp_c = c + 1 - 2 * yl
    sib = (sib_r, c)
    yhp = (yhp_r, c)
    ylp = (r, ylp_c)

    def xrow(d, h=None, k=None):
        return (yh if h is None else h) * 8 + lax.rem(x + d + 4, 4) * 2 + (core if k is None else k)

    def zcol(d, l=None):
        return lax.rem(z + d + 4, 4) * 2 + (yl if l is None else l)

    barrier = pltpu.get_barrier_semaphore()

    def greet_row(j, carry):
        pl.semaphore_signal(barrier, inc=1, device_id=(lax.rem(r + j, NR), c), device_id_type=MESH)
        return carry

    def greet_col(j, carry):
        pl.semaphore_signal(barrier, inc=1, device_id=(r, lax.rem(c + j, NC)), device_id_type=MESH)
        return carry

    lax.fori_loop(1, NR, greet_row, 0)
    lax.fori_loop(1, NC, greet_col, 0)
    pl.semaphore_wait(barrier, NR - 1 + NC - 1)

    def gather(t, value):
        vc[t, r] = value
        vr[t, c] = value
        sends = []

        def send(buf, slot, dev, k):
            cp = rcopy(buf.at[t, slot], buf.at[t, slot], ag_s.at[t, k], ag_r.at[t, k], dev)
            cp.start()
            sends.append(cp)

        def arrived(buf, slot, k):
            rcopy(buf.at[t, slot], buf.at[t, slot], ag_s.at[t, k], ag_r.at[t, k], sib).wait_recv()

        send(vr, c, ylp, 5)
        send(vc, r, yhp, 1)
        for d in (2, 1, 3):
            send(vc, r, (xrow(d), c), 1 + d)
            send(vr, c, (r, zcol(d)), 5 + d)
        send(vc, r, sib, 0)
        arrived(vr, ylp_c, 5)
        for d in (2, 1, 3):
            send(vr, ylp_c, (r, zcol(d)), 11 + d)
        arrived(vc, yhp_r, 1)
        for d in (2, 1, 3):
            send(vc, yhp_r, (xrow(d), c), 8 + d)
        send(vc, yhp_r, sib, 15)
        for d in (1, 3, 2):
            arrived(vc, xrow(-d), 1 + d)
            send(vc, xrow(-d), sib, 15 + d)
        for d in (1, 3, 2):
            arrived(vc, xrow(-d, h=1 - yh), 8 + d)
            send(vc, xrow(-d, h=1 - yh), sib, 18 + d)
        for d in (1, 3, 2):
            arrived(vr, zcol(-d), 5 + d)
        for d in (1, 3, 2):
            arrived(vr, zcol(-d, l=1 - yl), 11 + d)

        def finish():
            other = 1 - core
            arrived(vc, sib_r, 0)
            arrived(vc, xrow(0, h=1 - yh, k=other), 15)
            for d in (1, 3, 2):
                arrived(vc, xrow(-d, k=other), 15 + d)
            for d in (1, 3, 2):
                arrived(vc, xrow(-d, h=1 - yh, k=other), 18 + d)

        return sends, finish

    def onsite_part(value):
        return jnp.concatenate(
            [
                jnp.dot(onsite[p], value[p * BS : (p + 1) * BS], preferred_element_type=F32)
                for p in range(PB)
            ],
            axis=0,
        )

    centre = 0.5 * (top[0] + low[0])
    halfwidth = 0.5 * (top[0] - low[0])
    prev[...] = jnp.zeros_like(prev)
    cur[...] = y0[...]

    def degree(t, carry):
        value = cur[...].astype(BF16)
        sends, finish = gather(t, value)

        row_set = vr[t].reshape(NC * LR, K)
        for d in (2, 1, 3, 0):
            for h in range(2):
                at = pl.multiple_of(xrow(d, h=h, k=1 - core) * LR, LR)
                ms[t, d, h] = jnp.dot(tile_t[pl.ds(at, LR), :], row_set, preferred_element_type=F32)
            cp = rcopy(ms.at[t, d], sr.at[t, d], rs_s.at[t, d], rs_r.at[t, d], sib)
            cp.start()
            sends.append(cp)
        for d in (2, 1, 3, 0):
            rcopy(ms.at[t, d], sr.at[t, d], rs_s.at[t, d], rs_r.at[t, d], sib).wait_recv()
            for h in range(2):
                at = pl.multiple_of(xrow(d, h=h) * LR, LR)
                mx[t, d, h] = sr[t, d, h] + jnp.dot(
                    tile_t[pl.ds(at, LR), :], row_set, preferred_element_type=F32
                )
            if d:
                cp = rcopy(
                    mx.at[t, d], xr.at[t, d - 1], rs_s.at[t, 3 + d], rs_r.at[t, 3 + d], (xrow(d), c)
                )
                cp.start()
                sends.append(cp)
        finish()
        portion = vc[t].reshape(NR * LR, K)
        for d in (2, 1, 3, 0):
            at = pl.multiple_of(zcol(d, l=0) * LR, 2 * LR)
            zs[t, d] = jnp.dot(
                tile[pl.ds(at, 2 * LR), :], portion, preferred_element_type=F32
            ).reshape(2, LR, K)
            if d:
                cp = rcopy(
                    zs.at[t, d], zr.at[t, d - 1], rs_s.at[t, 6 + d], rs_r.at[t, 6 + d], (r, zcol(d))
                )
                cp.start()
                sends.append(cp)
        own = onsite_part(value)

        for d in (1, 3, 2):
            rcopy(mx.at[t, d], xr.at[t, d - 1], rs_s.at[t, 3 + d], rs_r.at[t, 3 + d], sib).wait_recv()
        ys[t] = (mx[t, 0, 1 - yh] + xr[t, 0, 1 - yh]) + (xr[t, 1, 1 - yh] + xr[t, 2, 1 - yh])
        cp_y = rcopy(ys.at[t], yr.at[t], rs_s.at[t, 10], rs_r.at[t, 10], yhp)
        cp_y.start()
        for d in (1, 3, 2):
            rcopy(zs.at[t, d], zr.at[t, d - 1], rs_s.at[t, 6 + d], rs_r.at[t, 6 + d], sib).wait_recv()
        ls[t] = (zs[t, 0, 1 - yl] + zr[t, 0, 1 - yl]) + (zr[t, 1, 1 - yl] + zr[t, 2, 1 - yl])
        cp_l = rcopy(ls.at[t], lr.at[t], rs_s.at[t, 11], rs_r.at[t, 11], ylp)
        cp_l.start()
        own += (mx[t, 0, yh] + xr[t, 0, yh]) + (xr[t, 1, yh] + xr[t, 2, yh])
        own += (zs[t, 0, yl] + zr[t, 0, yl]) + (zr[t, 1, yl] + zr[t, 2, yl])
        cp_y.wait_recv()
        own += yr[t]
        cp_l.wait_recv()
        own += lr[t]
        scale = jnp.where(t == 0, 1.0, 2.0).astype(F32)
        now = cur[...]
        following = scale * (own - centre * now) / halfwidth - prev[...]
        prev[...] = now
        cur[...] = following
        for cp in sends:
            cp.wait_send()
        cp_y.wait_send()
        cp_l.wait_send()
        return carry

    lax.fori_loop(0, DEG, degree, 0)
    y_out[...] = cur[...]
    rounded = cur[...].astype(BF16)
    out = (gram_out, ritz_out)

    def to_row(k):
        def step(j, carry):
            slab = pl.multiple_of(lax.rem(r + j, NR) * SLAB, SLAB)
            rcopy(
                part.at[k, pl.ds(slab, SLAB)], a1.at[k, j - 1], ar_s.at[k, 0, j], ar_r.at[k, 0, j],
                (lax.rem(r + j, NR), c),
            ).start()
            return carry

        lax.fori_loop(1, NR, step, 0)

    mine = pl.multiple_of(r * SLAB, SLAB)

    def to_col(k):
        def take(j, total):
            rcopy(
                a1.at[k, j - 1], a1.at[k, j - 1], ar_s.at[k, 0, j], ar_r.at[k, 0, j], sib
            ).wait_recv()
            return total + a1[k, j - 1]

        s2[k] = lax.fori_loop(1, NR, take, part[k, pl.ds(mine, SLAB), :])

        def step(j, carry):
            rcopy(
                s2.at[k], a2.at[k, j - 1], ar_s.at[k, 1, j], ar_r.at[k, 1, j],
                (r, lax.rem(c + j, NC)),
            ).start()
            return carry

        lax.fori_loop(1, NC, step, 0)

    def spread(k):
        def place(j, carry):
            rcopy(
                a2.at[k, j - 1], a2.at[k, j - 1], ar_s.at[k, 1, j], ar_r.at[k, 1, j], sib
            ).wait_recv()
            return carry

        lax.fori_loop(1, NC, place, 0)
        total = jnp.zeros((SLAB, K), F32)
        for i in range(NC):
            j = lax.rem(c - i + NC, NC)
            other = a2[k, jnp.maximum(j - 1, 0)]
            total = total + jnp.where(j == 0, s2[k], other)
        out[k][pl.ds(mine, SLAB), :] = total

        def step(j, carry):
            rcopy(
                out[k].at[pl.ds(mine, SLAB)], out[k].at[pl.ds(mine, SLAB)],
                ar_s.at[k, 2, j], ar_r.at[k, 2, j], (lax.rem(r + j, NR), c),
            ).start()
            return carry

        lax.fori_loop(1, NR, step, 0)

    def collect(k):
        def step(j, carry):
            there = pl.multiple_of(lax.rem(r - j + NR, NR) * SLAB, SLAB)
            rcopy(
                out[k].at[pl.ds(there, SLAB)], out[k].at[pl.ds(there, SLAB)],
                ar_s.at[k, 2, j], ar_r.at[k, 2, j], sib,
            ).wait_recv()
            return carry

        lax.fori_loop(1, NR, step, 0)

    def settle(k):
        def step(phase):
            def inner(j, carry):
                rcopy(
                    s2.at[k], s2.at[k], ar_s.at[k, phase, j], ar_r.at[k, phase, j], sib
                ).wait_send()
                return carry

            return inner

        lax.fori_loop(1, NR, step(0), 0)
        lax.fori_loop(1, NC, step(1), 0)
        lax.fori_loop(1, NR, step(2), 0)

    part[0] = contract_rows(rounded, rounded)
    to_row(0)
    sends, finish = gather(DEG, rounded)
    to_col(0)
    own = 0.5 * onsite_part(rounded)
    total = jnp.zeros((K, K), F32)

    def three(rows, image):
        high = image.astype(BF16)
        rest = image - high.astype(F32)
        mid = rest.astype(BF16)
        tail = (rest - mid.astype(F32)).astype(BF16)
        return contract_rows(rows, high) + (contract_rows(rows, mid) + contract_rows(rows, tail))

    finish()
    portion = vc[DEG].reshape(NR * LR, K)
    part[1] = three(rounded, own)
    for i in range(NC // 2):
        image = jnp.dot(tile[i * 2 * LR : (i + 1) * 2 * LR, :], portion, preferred_element_type=F32)
        part[1] += three(vr[DEG, 2 * i : 2 * i + 2].reshape(2 * LR, K), image)
    to_row(1)
    spread(0)
    to_col(1)
    collect(0)
    spread(1)
    collect(1)
    for cp in sends:
        cp.wait_send()
    settle(0)
    settle(1)


def local(orbitals_in, hblocks, block_cols, live_counts, onsite, cut_low, top_bound):
    dense_tile = build_tile(hblocks, block_cols, live_counts, NR * PB)
    vmem = pl.BlockSpec(memory_space=pltpu.VMEM)
    smem = pl.BlockSpec(memory_space=pltpu.SMEM)
    block = (LR, K)
    dma = pltpu.SemaphoreType.DMA
    current, gram_total, half_total = pl.pallas_call(
        kernel,
        out_shape=(
            jax.ShapeDtypeStruct(block, F32),
            jax.ShapeDtypeStruct((K, K), F32),
            jax.ShapeDtypeStruct((K, K), F32),
        ),
        in_specs=[vmem, vmem, vmem, vmem, smem, smem],
        out_specs=(vmem, vmem, vmem),
        scratch_shapes=[
            pltpu.VMEM((DEG + 1, NR) + block, BF16),
            pltpu.VMEM((DEG + 1, NC) + block, BF16),
            pltpu.VMEM((DEG, 4, 2) + block, F32),
            pltpu.VMEM((DEG, 4, 2) + block, F32),
            pltpu.VMEM((DEG, 4, 2) + block, F32),
            pltpu.VMEM((DEG, 3, 2) + block, F32),
            pltpu.VMEM((DEG, 4, 2) + block, F32),
            pltpu.VMEM((DEG, 3, 2) + block, F32),
            pltpu.VMEM((DEG,) + block, F32),
            pltpu.VMEM((DEG,) + block, F32),
            pltpu.VMEM((DEG,) + block, F32),
            pltpu.VMEM((DEG,) + block, F32),
            pltpu.VMEM(block, F32),
            pltpu.VMEM(block, F32),
            pltpu.VMEM((2, K, K), F32),
            pltpu.VMEM((2, NR - 1, SLAB, K), F32),
            pltpu.VMEM((2, SLAB, K), F32),
            pltpu.VMEM((2, NC - 1, SLAB, K), F32),
            dma((DEG + 1, 22)),
            dma((DEG + 1, 22)),
            dma((DEG, 12)),
            dma((DEG, 12)),
            dma((2, 3, NR)),
            dma((2, 3, NR)),
        ],
        compiler_params=pltpu.CompilerParams(
            collective_id=0, has_side_effects=True, vmem_limit_bytes=60 * 1024 * 1024
        ),
        name="filter_and_project",
    )(dense_tile, dense_tile.T, orbitals_in, onsite.reshape(PB, BS, BS), cut_low, top_bound)
    total_rows = NR * NC * LR
    gram_matrix = gram_total / total_rows
    ritz_matrix = (half_total + half_total.T) / total_rows
    factor = jnp.linalg.cholesky(gram_matrix)
    orbitals = jax.scipy.linalg.solve_triangular(factor, current.T, lower=True).T
    inner = jax.scipy.linalg.solve_triangular(factor, ritz_matrix, lower=True)
    projected = jax.scipy.linalg.solve_triangular(factor, inner.T, lower=True)
    return (orbitals, projected)


def solution(mesh):
    placed = (
        P(("row", "col"), None),
        P("row", "col", None),
        P("row", "col"),
        P("row", "col"),
        P(("row", "col"), None),
        P(),
        P(),
    )
    return jax.shard_map(
        local, mesh=mesh, in_specs=placed, out_specs=(P(("row", "col"), None), P()), check_vma=False
    )
```

time: 904 us -> 255 us (0.28)
  waiting for transfers between devices: 641 us -> 0 us
  Pallas kernels: 0 us -> 151 us
  blocking collectives: 102 us -> 0 us
  matrix products: 52.9 us -> 12.2 us
  between operations: 16.8 us -> 3.49 us
  other arithmetic: 64.7 us -> 54.8 us
    reduce_scatter x8 -> x0, waiting for transfers between devices: 424 us -> none  [the longest x4 265 us: apply(): lax.psum_scatter(mirror_rows(dense_tile, lax.all_gather(rounded, 'col', a...]
    psum x1 -> x0, waiting for transfers between devices: 153 us -> none  [local(): gram_total, cross_total = lax.psum((gram_part, cross_part), ('row', 'col'))]
    pallas_call x0 -> x1, Pallas kernels: none -> 151 us  [local(): pl.pallas_call(kernel, out_shape=(jax.ShapeDtypeStruct(block, F32), jax.S...]
    all_gather x4 -> x0, blocking collectives: 102 us -> none  [apply(): lax.all_gather(rounded, 'col', axis=0, tiled=True)]
    all_gather x4 -> x0, waiting for transfers between devices: 64.1 us -> none  [apply(): lax.all_gather(rounded, 'row', axis=0, tiled=True)]
    dot_general x14 -> x0, matrix products: 40.8 us -> none  [the longest x4 19.4 us: mirror_rows(): lax.dot_general(dense_tile, row_set, (((0,), (0,)), ((), ())), preferred_...]
    reshape x1 -> x2, local copies, waits for them, and re-layouts: 12.4 us -> 18.7 us  [build_tile(): dense_tile.astype(jnp.bfloat16).reshape(row_blocks * BS, column_blocks * BS)]
    another operation x7 -> x6, other arithmetic: 34.7 us -> 34 us  [local(): factor = jnp.linalg.cholesky(gram_matrix)]
  transfers between devices with their start and end apart: 13 -> 0, of which waited for: 12 -> 0; matrix products, arithmetic and copies ran while one was open for 8% -> 0% of each run, Pallas kernels for 0% -> 0%
where the time goes in v1:
time: 255 us; the launch traced here: 254 us
  Pallas kernels  151 us (59%)
  other arithmetic  54.8 us (21%)
  local copies, waits for them, and re-layouts  32.7 us (13%)
  matrix products  12.2 us (5%)
  between operations  3.49 us (1%)
    pallas_call x1, Pallas kernels, local(): pl.pallas_call(kernel, out_shape=(jax.ShapeDtypeStruct(block, F32), jax.S...  151 us
    another operation x6, other arithmetic, local(): factor = jnp.linalg.cholesky(gram_matrix)  34 us
    another operation x3, other arithmetic, local(): jax.scipy.linalg.solve_triangular(factor, current.T, lower=True)  19.9 us
    reshape x2, local copies, waits for them, and re-layouts, build_tile(): dense_tile.astype(jnp.bfloat16).reshape(row_blocks * BS, column_blocks * BS)  18.7 us
    dot_general x1, matrix products, build_tile(): jnp.einsum('isc,isab->iacb', selector.astype(jnp.bfloat16), blocks, prefe...  8.86 us
    reshape x1, local copies, waits for them, and re-layouts, build_tile(): blocks = hblocks.reshape(row_blocks, slot_count, BS, BS)  6.9 us

profile of v1, /device:TPU:1, one launch (start us, length us, event | category | flops | bytes accessed | tf_op | source)
XLA Modules:
  0.0 254.3 jit_solution(7200198218072016603)
XLA Ops:
  0.7 6.9 %reshape.59 = bf16[16,16,64,64]{3,2,1,0:T(8,128)(2,1)} reshape(bf16[16,16,4096]{2,1,0:T(8,128)(2,1)} %param.10) | data formatting | bytes 4194304 | tf_op jit(solution)/shard_map/reshape | solution.py:28
  7.6 8.9 %convert_bitcast_fusion = bf16[16,64,32,64]{3,2,1,0:T(8,128)(2,1)} fusion(bf16[16,16,64,64]{3,2,1,0:T(8,128)(2,1)} %reshape.59, s32[16,16]{1,0:T(8,128)S(1)} %copy-done.3, pred[16,16]{1,0:T(8,128)(4,1)S(1)} %iota_compare_fusion.4), kind=kOutput, calls=%fused_computation.2 | convolution fusion | flops 69222400 | bytes 6292736 | tf_op jit(solution)/shard_map/isc,isab->iacb/dot_general | solution.py:29
  16.5 12.3 %reshape.104.tile = bf16[1024,2048]{1,0:T(8,128)(2,1)} reshape(bf16[16,64,32,64]{3,2,1,0:T(8,128)(2,1)} %convert_bitcast_fusion) | data formatting | bytes 8388608 | tf_op jit(solution)/shard_map/reshape | solution.py:32
  28.8 6.4 %copy.17 = bf16[1024,2048]{0,1:T(8,128)(2,1)} copy(bf16[1024,2048]{1,0:T(8,128)(2,1)} %reshape.104.tile) | data formatting | bytes 8388608 | tf_op jit(solution)/shard_map/reshape | solution.py:32
  35.2 0.7 reshape.61.onsite
  37.2 151.1 %filter_and_project.1 = (f32[128,256]{1,0:T(8,128)}, f32[256,256]{1,0:T(8,128)}, f32[256,256]{1,0:T(8,128)}) custom-call(bf16[1024,2048]{1,0:T(8,128)(2,1)} %reshape.104.tile, bf16[2048,1024]{1,0:T(8,128)(2,1)} %bitcast.69, f32[128,256]{1,0:T(8,128)} %y0.1, bf16[2,64,64]{2,1,0:T(8,128)(2,1)} %reshape.61.onsite, f32[1]{0:T(128)S(6)} %copy.30.low, f32[1]{0:T(128)S(6)} %copy.31.top), custom_call_target="tpu_custom_call" | custom-call | tf_op jit(solution)/shard_map/filter_and_project/pallas_call | solution.py:336
  188.4 1.1 copy.12
  189.7 11.7 %cholesky.50 = f32[128,128]{1,0:T(8,128)S(1)} custom-call(f32[128,128]{1,0:T(8,128)S(1)} %cholesky.118), custom_call_target="Cholesky" | custom-call | tf_op jit(solution)/shard_map/jit(cholesky)/cholesky | solution.py:379
  201.5 9.8 %custom-call.18 = f32[1,128,128]{1,2,0:T(8,128)S(1)} custom-call(f32[1,128,128]{2,1,0:T(8,128)S(1)} %get-tuple-element.48), custom_call_target="InvertDiagBlocksLowerTriangular" | custom-call | tf_op jit(solution)/shard_map/jit(cholesky)/cholesky | solution.py:379
  211.8 11.7 %cholesky.105 = f32[128,128]{1,0:T(8,128)S(1)} custom-call(f32[128,128]{1,0:T(8,128)S(1)} %convolution_subtract_fusion.3), custom_call_target="Cholesky" | custom-call | tf_op jit(solution)/shard_map/jit(cholesky)/cholesky | solution.py:379
  223.5 0.6 compare_reduce_fusion
  225.6 4.1 %while.5 = (s32[]{:T(128)}, f32[256,256]{1,0:T(8,128)S(1)}, s32[2,2]{1,0:T(2,128)S(1)}, f32[2,128,128]{2,1,0:T(8,128)S(1)}, s32[]{:T(128)}) while((s32[]{:T(128)}, f32[256,256]{1,0:T(8,128)S(1)}, s32[2,2]{1,0:T(2,128)S(1)}, f32[2,128,128]{2,1,0:T(8,128)S(1)}, s32[]{:T(128)}) %tuple.36), condition=%wide.while_cond.1, body=%wide.while_body.1.sunk | while | flops 2 | bytes 131181 | solution.py:380
  225.6 0.6 fusion.33
  226.2 1.4 bitcast_dynamic-update-slice_fusion.2
  227.7 0.6 fusion.33
  228.3 1.4 bitcast_dynamic-update-slice_fusion.2
  229.7 19.9 %custom-call.19 = f32[2,128,128]{1,2,0:T(8,128)S(1)} custom-call(f32[2,128,128]{2,1,0:T(8,128)S(1)} %get-tuple-element.24), custom_call_target="InvertDiagBlocksLowerTriangular" | custom-call | tf_op jit(solution)/shard_map/jit(_solve_triangular)/triangular_solve | solution.py:380
  250.1 0.4 convolution_subtract_fusion.1
  250.5 0.3 fusion.18
  250.9 0.3 fusion.3
  251.2 0.4 convolution_subtract_fusion
  251.6 0.3 fusion.17
  251.9 0.7 pad_maximum_fusion
  253.5 0.8 copy.15
  (34 shorter events, 2.3 us)
Async XLA Ops:
  0.6 6.9 %copy-start.4 = (s32[16,1]{0,1:T(1,128)S(1)}, s32[16,1]{0,1:T(1,128)}, u32[]{:S(2)}) copy-start(s32[16,1]{0,1:T(1,128)} %param.12) | copy-start | bytes 196
  0.6 7.0 %copy-start.3 = (s32[16,16]{1,0:T(8,128)S(1)}, s32[16,16]{1,0:T(8,128)}, u32[]{:S(2)}) copy-start(s32[16,16]{1,0:T(8,128)} %param.11) | copy-start | bytes 3076
  28.8 6.4 %copy-start.2 = (bf16[2,4096]{1,0:T(2,128)(2,1)S(1)}, bf16[2,4096]{1,0:T(2,128)(2,1)}, u32[]{:S(2)}) copy-start(bf16[2,4096]{1,0:T(2,128)(2,1)} %param.13) | copy-start | bytes 49156
  188.3 61.3 %copy-start = (f32[256,256]{1,0:T(8,128)S(1)}, f32[256,256]{1,0:T(8,128)}, u32[]{:S(2)}) copy-start(f32[256,256]{1,0:T(8,128)} %get-tuple-element.8) | copy-start | bytes 786436
  189.5 63.1 %copy-start.1 = (f32[128,256]{1,0:T(8,128)S(1)}, f32[128,256]{1,0:T(8,128)}, u32[]{:S(2)}) copy-start(f32[128,256]{1,0:T(8,128)} %get-tuple-element.7) | copy-start | bytes 393220

commit v2 on v1

--- a/solution.py
+++ b/solution.py
@@ -17,6 +17,9 @@
 NR = 16
 NC = 8
 SLAB = K // NR
+CB = 64
+STEP = 8
+HIGH = lax.Precision.HIGHEST
 
 
 def build_tile(hblocks, block_cols, live_counts, column_blocks):
@@ -325,6 +328,72 @@
         cp.wait_send()
     settle(0)
     settle(1)
+
+
+def dot_f32(a, b, left, right):
+    return lax.dot_general(a, b, (((left,), (right,)), ((), ())), precision=HIGH, preferred_element_type=F32)
+
+
+def dot_nn(a, b):
+    return dot_f32(a, b, 1, 0)
+
+
+def dot_nt(a, b):
+    return dot_f32(a, b, 1, 1)
+
+
+def dot_tn(a, b):
+    return dot_f32(a, b, 0, 0)
+
+
+def inverse_factor(block):
+    rows = lax.broadcasted_iota(jnp.int32, (CB, 2 * CB), 0)
+    lanes = lax.broadcasted_iota(jnp.int32, (CB, 2 * CB), 1)
+    unit = jnp.where(lanes == rows + CB, 1.0, 0.0).astype(F32)
+    x = jnp.where(lanes < CB, jnp.concatenate([block, block], axis=1), unit)
+    for s in range(0, CB, STEP):
+        col = [jnp.broadcast_to(x[:, s + j : s + j + 1], (CB, 2 * CB)) for j in range(STEP)]
+        row = [x[s + j : s + j + 1, :] for j in range(STEP)]
+        for j in range(STEP):
+            d = col[j][s + j : s + j + 1, :]
+            q = lax.rsqrt(d)
+            col[j] = col[j] * q
+            row[j] = row[j] * q
+            for m in range(j + 1, STEP):
+                f = col[j][s + m : s + m + 1, :]
+                col[m] = col[m] - col[j] * f
+                row[m] = row[m] - row[j] * f
+        change = col[0] * row[0]
+        for j in range(1, STEP):
+            change = change + col[j] * row[j]
+        x = jnp.where(rows >= s + STEP, x - change, x)
+        for j in range(STEP):
+            x = jnp.where(rows == s + j, row[j], x)
+    return x[:, CB:]
+
+
+def invert(a, b):
+    b[...] = jnp.zeros_like(b)
+    for k in range(0, K, CB):
+        e = k + CB
+        inv = inverse_factor(a[k:e, k:e])
+        if k:
+            b[k:e, :k] = dot_nn(inv, b[k:e, :k])
+        b[k:e, k:e] = inv
+        if e < K:
+            u = dot_nn(inv, a[k:e, e:])
+            a[e:, e:] = a[e:, e:] - dot_tn(u, u)
+            b[e:, :e] = b[e:, :e] - dot_tn(u, b[k:e, :e])
+
+
+def finish_kernel(cur, gram, half, orb, proj, a, b):
+    scale = 1.0 / (NR * NC * LR)
+    a[...] = gram[...] * scale
+    invert(a, b)
+    w = b[...]
+    orb[...] = dot_nt(cur[...], w)
+    s = half[...] * scale
+    proj[...] = dot_nt(dot_nn(w, s) + dot_nt(w, s), w)
 
 
 def local(orbitals_in, hblocks, block_cols, live_counts, onsite, cut_low, top_bound):
@@ -373,14 +442,12 @@
         ),
         name="filter_and_project",
     )(dense_tile, dense_tile.T, orbitals_in, onsite.reshape(PB, BS, BS), cut_low, top_bound)
-    total_rows = NR * NC * LR
-    gram_matrix = gram_total / total_rows
-    ritz_matrix = (half_total + half_total.T) / total_rows
-    factor = jnp.linalg.cholesky(gram_matrix)
-    orbitals = jax.scipy.linalg.solve_triangular(factor, current.T, lower=True).T
-    inner = jax.scipy.linalg.solve_triangular(factor, ritz_matrix, lower=True)
-    projected = jax.scipy.linalg.solve_triangular(factor, inner.T, lower=True)
-    return (orbitals, projected)
+    return pl.pallas_call(
+        finish_kernel,
+        out_shape=(jax.ShapeDtypeStruct(block, F32), jax.ShapeDtypeStruct((K, K), F32)),
+        scratch_shapes=[pltpu.VMEM((K, K), F32)] * 2,
+        name="orthonormalize",
+    )(current, gram_total, half_total)
 
 
 def solution(mesh):

time: 255 us -> 201 us (0.79)
  other arithmetic: 54.8 us -> 0.07 us
  Pallas kernels: 151 us -> 163 us
  local copies, waits for them, and re-layouts: 32.7 us -> 26.4 us
  matrix products: 12.2 us -> 8.87 us
    another operation x10 -> x0, other arithmetic: 54.6 us -> none  [the longest x6 34 us: local(): factor = jnp.linalg.cholesky(gram_matrix)]
    pallas_call x0 -> x1, Pallas kernels: none -> 12.3 us  [local(): pl.pallas_call(finish_kernel, out_shape=(jax.ShapeDtypeStruct(block, F32)...]
    another operation x9 -> x0, local copies, waits for them, and re-layouts: 4.16 us -> none
    another operation x11 -> x0, matrix products: 3.35 us -> none  [the longest x3 1.01 us: local(): projected = jax.scipy.linalg.solve_triangular(factor, inner.T, lower=True)]
where the time goes in v2:
time: 201 us
  Pallas kernels  163 us (81%)
  local copies, waits for them, and re-layouts  26.4 us (13%)
  matrix products  8.87 us (4%)
    pallas_call x1, Pallas kernels, local(): pl.pallas_call(kernel, out_shape=(jax.ShapeDtypeStruct(block, F32), jax.S...  151 us
    reshape x2, local copies, waits for them, and re-layouts, build_tile(): dense_tile.astype(jnp.bfloat16).reshape(row_blocks * BS, column_blocks * BS)  18.7 us
    pallas_call x1, Pallas kernels, local(): pl.pallas_call(finish_kernel, out_shape=(jax.ShapeDtypeStruct(block, F32)...  12.3 us
    dot_general x1, matrix products, build_tile(): jnp.einsum('isc,isab->iacb', selector.astype(jnp.bfloat16), blocks, prefe...  8.87 us
    reshape x1, local copies, waits for them, and re-layouts, build_tile(): blocks = hblocks.reshape(row_blocks, slot_count, BS, BS)  6.89 us

profile of v2, /device:TPU:1, one launch (start us, length us, event | category | flops | bytes accessed | tf_op | source)
XLA Modules:
  0.0 200.6 jit_solution(7905839069164400439)
XLA Ops:
  0.6 0.0 copy-start.2
  0.6 0.0 copy-start.1
  0.7 6.9 %reshape.36 = bf16[16,16,64,64]{3,2,1,0:T(8,128)(2,1)} reshape(bf16[16,16,4096]{2,1,0:T(8,128)(2,1)} %param.8) | data formatting | bytes 4194304 | tf_op jit(solution)/shard_map/reshape | solution.py:31
  7.5 0.0 copy-done.2
  7.5 0.1 iota_compare_fusion.1
  7.6 0.0 copy-done.1
  7.6 8.9 %convert_bitcast_fusion = bf16[16,64,32,64]{3,2,1,0:T(8,128)(2,1)} fusion(bf16[16,16,64,64]{3,2,1,0:T(8,128)(2,1)} %reshape.36, s32[16,16]{1,0:T(8,128)S(1)} %copy-done.1, pred[16,16]{1,0:T(8,128)(4,1)S(1)} %iota_compare_fusion.1), kind=kOutput, calls=%fused_computation | convolution fusion | flops 69222400 | bytes 6292736 | tf_op jit(solution)/shard_map/isc,isab->iacb/dot_general | solution.py:32
  16.5 12.3 %reshape.40.tile = bf16[1024,2048]{1,0:T(8,128)(2,1)} reshape(bf16[16,64,32,64]{3,2,1,0:T(8,128)(2,1)} %convert_bitcast_fusion) | data formatting | bytes 8388608 | tf_op jit(solution)/shard_map/reshape | solution.py:35
  28.8 0.0 copy-start
  28.8 6.4 %copy.13 = bf16[1024,2048]{0,1:T(8,128)(2,1)} copy(bf16[1024,2048]{1,0:T(8,128)(2,1)} %reshape.40.tile) | data formatting | bytes 8388608 | tf_op jit(solution)/shard_map/reshape | solution.py:35
  35.2 0.0 copy-done
  35.2 0.7 reshape.38.onsite
  37.2 151.1 %filter_and_project.1 = (f32[128,256]{1,0:T(8,128)}, f32[256,256]{1,0:T(8,128)}, f32[256,256]{1,0:T(8,128)}) custom-call(bf16[1024,2048]{1,0:T(8,128)(2,1)} %reshape.40.tile, bf16[2048,1024]{1,0:T(8,128)(2,1)} %bitcast.11, f32[128,256]{1,0:T(8,128)} %y0.1, bf16[2,64,64]{2,1,0:T(8,128)(2,1)} %reshape.38.onsite, f32[1]{0:T(128)S(6)} %copy.16.low, f32[1]{0:T(128)S(6)} %copy.17.top), custom_call_target="tpu_custom_call" | custom-call | tf_op jit(solution)/shard_map/filter_and_project/pallas_call | solution.py:405
  188.4 12.3 %orthonormalize.1 = (f32[128,256]{1,0:T(8,128)}, f32[256,256]{1,0:T(8,128)}) custom-call(f32[128,256]{1,0:T(8,128)} %get-tuple-element.5.cur, f32[256,256]{1,0:T(8,128)} %get-tuple-element.6.gram, f32[256,256]{1,0:T(8,128)} %get-tuple-element.7.half), custom_call_target="tpu_custom_call" | custom-call | tf_op jit(solution)/shard_map/orthonormalize/pallas_call | solution.py:445
Async XLA Ops:
  0.6 6.9 %copy-start.2 = (s32[16,1]{0,1:T(1,128)S(1)}, s32[16,1]{0,1:T(1,128)}, u32[]{:S(2)}) copy-start(s32[16,1]{0,1:T(1,128)} %param.10) | copy-start | bytes 196
  0.6 7.0 %copy-start.1 = (s32[16,16]{1,0:T(8,128)S(1)}, s32[16,16]{1,0:T(8,128)}, u32[]{:S(2)}) copy-start(s32[16,16]{1,0:T(8,128)} %param.9) | copy-start | bytes 3076
  28.8 6.4 %copy-start = (bf16[2,4096]{1,0:T(2,128)(2,1)S(1)}, bf16[2,4096]{1,0:T(2,128)(2,1)}, u32[]{:S(2)}) copy-start(bf16[2,4096]{1,0:T(2,128)(2,1)} %param.11) | copy-start | bytes 49156

commit v3 on v2

--- a/solution.py
+++ b/solution.py
@@ -22,34 +22,72 @@
 HIGH = lax.Precision.HIGHEST
 
 
-def build_tile(hblocks, block_cols, live_counts, column_blocks):
-    row_blocks, slot_count, _ = hblocks.shape
-    occupied = jnp.arange(slot_count, dtype=jnp.int32)[None, :] < live_counts
-    selector = (
-        block_cols[:, :, None] == jnp.arange(column_blocks, dtype=jnp.int32)[None, None, :]
-    ) & occupied[:, :, None]
-    blocks = hblocks.reshape(row_blocks, slot_count, BS, BS)
-    dense_tile = jnp.einsum(
-        "isc,isab->iacb", selector.astype(jnp.bfloat16), blocks, preferred_element_type=jnp.float32
-    )
-    return dense_tile.astype(jnp.bfloat16).reshape(row_blocks * BS, column_blocks * BS)
-
-
 def rcopy(src, dst, ssem, rsem, dev):
     return pltpu.make_async_remote_copy(
         src_ref=src, dst_ref=dst, send_sem=ssem, recv_sem=rsem, device_id=dev, device_id_type=MESH
     )
 
 
-def contract_rows(a, b):
-    return lax.dot_general(a, b, (((0,), (0,)), ((), ())), preferred_element_type=F32)
+def product(a, b, left, right):
+    return lax.dot_general(a, b, (((left,), (right,)), ((), ())), preferred_element_type=F32)
+
+
+def build(blocks, cols, live, pick, tile):
+    slots = lax.broadcasted_iota(jnp.int32, cols.shape, 1)
+    wanted = jnp.where(slots < live[...], cols[...], -9).astype(F32).astype(BF16)
+    count = cols.shape[1]
+    depth = 4 * 8 * count
+    lane = lax.broadcasted_iota(jnp.int32, (count, depth), 1)
+    row = lax.broadcasted_iota(jnp.int32, (count, depth), 0)
+    spread = jnp.where(lax.rem(lane, count) == row, 1.0, 0.0).astype(BF16)
+    column = product(wanted, spread, 1, 0)
+    column = column - lax.rem(lane // (8 * count), 2).astype(F32)
+
+    high = lax.broadcasted_iota(jnp.int32, pick.shape, 0)
+    deep = lax.broadcasted_iota(jnp.int32, pick.shape, 1)
+    match = lax.rem(high, 16) == 2 * lax.rem(deep // count, 8) + deep // (16 * count)
+    pick[...] = jnp.where(match, 2 * (high // 16), -99).astype(F32)
+    first = lax.broadcasted_iota(jnp.int32, (8 * count, 2 * BS), 1) < BS
+    none = jnp.zeros((8 * count, 2 * BS), BF16)
+    return column, first, none
+
+
+def build_row(i, blocks, column_ref, pick, first, none, tile):
+    place = jnp.where(pick[...] == column_ref[pl.ds(i, 1), :], 1.0, 0.0).astype(BF16)
+    for half in range(2):
+        sides = []
+        for p in (2 * half, 2 * half + 1):
+            at = [(p * 8 + m) * 2 * BS for m in range(8)]
+            plain = jnp.concatenate([blocks[i, :, a : a + 2 * BS] for a in at], axis=0)
+            swapped = jnp.concatenate([plain[:, BS:], plain[:, :BS]], axis=1)
+            sides.append(
+                jnp.concatenate(
+                    [
+                        jnp.where(first, plain, none),
+                        jnp.where(first, none, swapped),
+                        jnp.where(first, swapped, none),
+                        jnp.where(first, none, plain),
+                    ],
+                    axis=0,
+                )
+            )
+        rows = product(place, jnp.concatenate(sides, axis=1), 1, 0).astype(BF16)
+        for p in range(2):
+            at = pl.multiple_of(i * BS + (2 * half + p) * 16, 16)
+            for g in range(NR):
+                tile[pl.ds(at, 16), g * LR : (g + 1) * LR] = rows[
+                    g * 16 : (g + 1) * 16, p * LR : (p + 1) * LR
+                ]
 
 
 def kernel(
-    tile, tile_t, y0, onsite, low, top, y_out, gram_out, ritz_out,
+    hblocks, cols, live, y0, onsite, low, top, y_out, gram_out, ritz_out,
+    tile, blocks, pick, column, diag,
     vc, vr, ms, sr, mx, xr, zs, zr, ys, yr, ls, lr, prev, cur, part, a1, s2, a2,
-    ag_s, ag_r, rs_s, rs_r, ar_s, ar_r,
+    ag_s, ag_r, rs_s, rs_r, ar_s, ar_r, load,
 ):
+    fetch = pltpu.make_async_copy(hblocks, blocks, load)
+    fetch.start()
     r = lax.axis_index("row")
     c = lax.axis_index("col")
     core = lax.rem(r, 2)
@@ -70,6 +108,9 @@
     def zcol(d, l=None):
         return lax.rem(z + d + 4, 4) * 2 + (yl if l is None else l)
 
+    def part_of(buf, t, slot):
+        return buf.at[t, :, pl.ds(pl.multiple_of(slot * LR, LR), LR)]
+
     barrier = pltpu.get_barrier_semaphore()
 
     def greet_row(j, carry):
@@ -82,20 +123,30 @@
 
     lax.fori_loop(1, NR, greet_row, 0)
     lax.fori_loop(1, NC, greet_col, 0)
+
+    cur[...] = y0[...].T
+    prev[...] = jnp.zeros_like(prev)
+    diag[...] = jnp.zeros_like(diag)
+    for p in range(PB):
+        diag[p * BS : (p + 1) * BS, p * BS : (p + 1) * BS] = onsite[p]
     pl.semaphore_wait(barrier, NR - 1 + NC - 1)
 
-    def gather(t, value):
-        vc[t, r] = value
-        vr[t, c] = value
+    def gather(t, value, between=None):
+        vc[t, :, pl.ds(pl.multiple_of(r * LR, LR), LR)] = value
+        vr[t, :, pl.ds(pl.multiple_of(c * LR, LR), LR)] = value
         sends = []
 
         def send(buf, slot, dev, k):
-            cp = rcopy(buf.at[t, slot], buf.at[t, slot], ag_s.at[t, k], ag_r.at[t, k], dev)
+            cp = rcopy(
+                part_of(buf, t, slot), part_of(buf, t, slot), ag_s.at[t, k], ag_r.at[t, k], dev
+            )
             cp.start()
             sends.append(cp)
 
         def arrived(buf, slot, k):
-            rcopy(buf.at[t, slot], buf.at[t, slot], ag_s.at[t, k], ag_r.at[t, k], sib).wait_recv()
+            rcopy(
+                part_of(buf, t, slot), part_of(buf, t, slot), ag_s.at[t, k], ag_r.at[t, k], sib
+            ).wait_recv()
 
         send(vr, c, ylp, 5)
         send(vc, r, yhp, 1)
@@ -132,59 +183,75 @@
 
         return sends, finish
 
-    def onsite_part(value):
-        return jnp.concatenate(
-            [
-                jnp.dot(onsite[p], value[p * BS : (p + 1) * BS], preferred_element_type=F32)
-                for p in range(PB)
-            ],
-            axis=0,
-        )
-
     centre = 0.5 * (top[0] + low[0])
     halfwidth = 0.5 * (top[0] - low[0])
-    prev[...] = jnp.zeros_like(prev)
-    cur[...] = y0[...]
+
+    def settle_sends(sends):
+        for cp in sends:
+            cp.wait_send()
 
     def degree(t, carry):
         value = cur[...].astype(BF16)
         sends, finish = gather(t, value)
 
-        row_set = vr[t].reshape(NC * LR, K)
-        for d in (2, 1, 3, 0):
+        @pl.when(t == 0)
+        def _():
+            fetch.wait()
+            spread, first, none = build(blocks, cols, live, pick, tile)
+            column[...] = spread
+
+            def one(i, inner):
+                build_row(i, blocks, column, pick, first, none, tile)
+                return inner
+
+            lax.fori_loop(0, hblocks.shape[0], one, 0)
+
+        def mirror(d):
             for h in range(2):
-                at = pl.multiple_of(xrow(d, h=h, k=1 - core) * LR, LR)
-                ms[t, d, h] = jnp.dot(tile_t[pl.ds(at, LR), :], row_set, preferred_element_type=F32)
-            cp = rcopy(ms.at[t, d], sr.at[t, d], rs_s.at[t, d], rs_r.at[t, d], sib)
+                at = pl.multiple_of(xrow(d, h=h, k=0) * LR, 2 * LR)
+                both = product(vr[t], tile[:, pl.ds(at, 2 * LR)], 1, 0)
+                ms[t, d, 0, h] = both[:, :LR]
+                ms[t, d, 1, h] = both[:, LR:]
+            cp = rcopy(ms.at[t, d, 1 - core], sr.at[t, d], rs_s.at[t, d], rs_r.at[t, d], sib)
             cp.start()
             sends.append(cp)
-        for d in (2, 1, 3, 0):
-            rcopy(ms.at[t, d], sr.at[t, d], rs_s.at[t, d], rs_r.at[t, d], sib).wait_recv()
-            for h in range(2):
-                at = pl.multiple_of(xrow(d, h=h) * LR, LR)
-                mx[t, d, h] = sr[t, d, h] + jnp.dot(
-                    tile_t[pl.ds(at, LR), :], row_set, preferred_element_type=F32
-                )
+
+        def mirror_on(d):
+            rcopy(ms.at[t, d, core], sr.at[t, d], rs_s.at[t, d], rs_r.at[t, d], sib).wait_recv()
+            mx[t, d] = sr[t, d] + ms[t, d, core]
             if d:
                 cp = rcopy(
                     mx.at[t, d], xr.at[t, d - 1], rs_s.at[t, 3 + d], rs_r.at[t, 3 + d], (xrow(d), c)
                 )
                 cp.start()
                 sends.append(cp)
-        finish()
-        portion = vc[t].reshape(NR * LR, K)
-        for d in (2, 1, 3, 0):
+
+        def direct(d):
             at = pl.multiple_of(zcol(d, l=0) * LR, 2 * LR)
-            zs[t, d] = jnp.dot(
-                tile[pl.ds(at, 2 * LR), :], portion, preferred_element_type=F32
-            ).reshape(2, LR, K)
+            both = product(vc[t], tile[pl.ds(at, 2 * LR), :], 1, 1)
+            zs[t, d, 0] = both[:, :LR]
+            zs[t, d, 1] = both[:, LR:]
             if d:
                 cp = rcopy(
                     zs.at[t, d], zr.at[t, d - 1], rs_s.at[t, 6 + d], rs_r.at[t, 6 + d], (r, zcol(d))
                 )
                 cp.start()
                 sends.append(cp)
-        own = onsite_part(value)
+
+        mirror(2)
+        mirror(1)
+        finish()
+        mirror_on(2)
+        direct(2)
+        mirror_on(1)
+        mirror(3)
+        direct(1)
+        mirror_on(3)
+        direct(3)
+        mirror(0)
+        direct(0)
+        mirror_on(0)
+        own = product(value, diag[...], 1, 1)
 
         for d in (1, 3, 2):
             rcopy(mx.at[t, d], xr.at[t, d - 1], rs_s.at[t, 3 + d], rs_r.at[t, 3 + d], sib).wait_recv()
@@ -207,8 +274,7 @@
         following = scale * (own - centre * now) / halfwidth - prev[...]
         prev[...] = now
         cur[...] = following
-        for cp in sends:
-            cp.wait_send()
+        settle_sends(sends)
         cp_y.wait_send()
         cp_l.wait_send()
         return carry
@@ -298,34 +364,30 @@
         lax.fori_loop(1, NC, step(1), 0)
         lax.fori_loop(1, NR, step(2), 0)
 
-    part[0] = contract_rows(rounded, rounded)
+    part[0] = product(rounded, rounded, 1, 1)
     to_row(0)
     sends, finish = gather(DEG, rounded)
     to_col(0)
-    own = 0.5 * onsite_part(rounded)
-    total = jnp.zeros((K, K), F32)
 
     def three(rows, image):
         high = image.astype(BF16)
         rest = image - high.astype(F32)
         mid = rest.astype(BF16)
-        tail = (rest - mid.astype(F32)).astype(BF16)
-        return contract_rows(rows, high) + (contract_rows(rows, mid) + contract_rows(rows, tail))
+        low_part = (rest - mid.astype(F32)).astype(BF16)
+        return product(rows, high, 1, 1) + (product(rows, mid, 1, 1) + product(rows, low_part, 1, 1))
 
     finish()
-    portion = vc[DEG].reshape(NR * LR, K)
-    part[1] = three(rounded, own)
+    part[1] = three(rounded, 0.5 * product(rounded, diag[...], 1, 1))
     for i in range(NC // 2):
-        image = jnp.dot(tile[i * 2 * LR : (i + 1) * 2 * LR, :], portion, preferred_element_type=F32)
-        part[1] += three(vr[DEG, 2 * i : 2 * i + 2].reshape(2 * LR, K), image)
+        span = slice(i * 2 * LR, (i + 1) * 2 * LR)
+        part[1] += three(vr[DEG, :, span], product(vc[DEG], tile[span, :], 1, 1))
     to_row(1)
     spread(0)
     to_col(1)
     collect(0)
     spread(1)
     collect(1)
-    for cp in sends:
-        cp.wait_send()
+    settle_sends(sends)
     settle(0)
     settle(1)
 
@@ -391,16 +453,15 @@
     a[...] = gram[...] * scale
     invert(a, b)
     w = b[...]
-    orb[...] = dot_nt(cur[...], w)
+    orb[...] = dot_f32(cur[...], w, 0, 1)
     s = half[...] * scale
     proj[...] = dot_nt(dot_nn(w, s) + dot_nt(w, s), w)
 
 
 def local(orbitals_in, hblocks, block_cols, live_counts, onsite, cut_low, top_bound):
-    dense_tile = build_tile(hblocks, block_cols, live_counts, NR * PB)
     vmem = pl.BlockSpec(memory_space=pltpu.VMEM)
     smem = pl.BlockSpec(memory_space=pltpu.SMEM)
-    block = (LR, K)
+    block = (K, LR)
     dma = pltpu.SemaphoreType.DMA
     current, gram_total, half_total = pl.pallas_call(
         kernel,
@@ -409,12 +470,17 @@
             jax.ShapeDtypeStruct((K, K), F32),
             jax.ShapeDtypeStruct((K, K), F32),
         ),
-        in_specs=[vmem, vmem, vmem, vmem, smem, smem],
+        in_specs=[pl.BlockSpec(memory_space=pl.ANY), vmem, vmem, vmem, vmem, smem, smem],
         out_specs=(vmem, vmem, vmem),
         scratch_shapes=[
-            pltpu.VMEM((DEG + 1, NR) + block, BF16),
-            pltpu.VMEM((DEG + 1, NC) + block, BF16),
-            pltpu.VMEM((DEG, 4, 2) + block, F32),
+            pltpu.VMEM((NC * LR, NR * LR), BF16),
+            pltpu.VMEM(hblocks.shape, BF16),
+            pltpu.VMEM((NR * 16, 32 * hblocks.shape[1]), F32),
+            pltpu.VMEM((hblocks.shape[0], 32 * hblocks.shape[1]), F32),
+            pltpu.VMEM((LR, LR), BF16),
+            pltpu.VMEM((DEG + 1, K, NR * LR), BF16),
+            pltpu.VMEM((DEG + 1, K, NC * LR), BF16),
+            pltpu.VMEM((DEG, 4, 2, 2) + block, F32),
             pltpu.VMEM((DEG, 4, 2) + block, F32),
             pltpu.VMEM((DEG, 4, 2) + block, F32),
             pltpu.VMEM((DEG, 3, 2) + block, F32),
@@ -436,15 +502,16 @@
             dma((DEG, 12)),
             dma((2, 3, NR)),
             dma((2, 3, NR)),
+            dma,
         ],
         compiler_params=pltpu.CompilerParams(
-            collective_id=0, has_side_effects=True, vmem_limit_bytes=60 * 1024 * 1024
+            collective_id=0, has_side_effects=True, vmem_limit_bytes=62 * 1024 * 1024
         ),
         name="filter_and_project",
-    )(dense_tile, dense_tile.T, orbitals_in, onsite.reshape(PB, BS, BS), cut_low, top_bound)
+    )(hblocks, block_cols, live_counts, orbitals_in, onsite.reshape(PB, BS, BS), cut_low, top_bound)
     return pl.pallas_call(
         finish_kernel,
-        out_shape=(jax.ShapeDtypeStruct(block, F32), jax.ShapeDtypeStruct((K, K), F32)),
+        out_shape=(jax.ShapeDtypeStruct((LR, K), F32), jax.ShapeDtypeStruct((K, K), F32)),
         scratch_shapes=[pltpu.VMEM((K, K), F32)] * 2,
         name="orthonormalize",
     )(current, gram_total, half_total)

time: 201 us -> 171 us (0.85)
  local copies, waits for them, and re-layouts: 26.4 us -> 2.76 us
  matrix products: 8.87 us -> 0 us
  Pallas kernels: 163 us -> 166 us
    reshape x3 -> x0, local copies, waits for them, and re-layouts: 25.6 us -> none  [the longest x2 18.7 us: build_tile(): dense_tile.astype(jnp.bfloat16).reshape(row_blocks * BS, column_blocks * BS)]
    dot_general x1 -> x0, matrix products: 8.87 us -> none  [build_tile(): jnp.einsum('isc,isab->iacb', selector.astype(jnp.bfloat16), blocks, prefe...]
    pallas_call x1, Pallas kernels: 151 us -> 154 us  [local(): pl.pallas_call(kernel, out_shape=(jax.ShapeDtypeStruct(block, F32), jax.S...]
where the time goes in v3:
time: 171 us
  Pallas kernels  166 us (97%)
  local copies, waits for them, and re-layouts  2.76 us (2%)
  between operations  1.93 us (1%)
    pallas_call x1, Pallas kernels, local(): pl.pallas_call(kernel, out_shape=(jax.ShapeDtypeStruct(block, F32), jax.S...  154 us
    pallas_call x1, Pallas kernels, local(): pl.pallas_call(finish_kernel, out_shape=(jax.ShapeDtypeStruct((LR, K), F3...  12.3 us

profile of v3, /device:TPU:1, one launch (start us, length us, event | category | flops | bytes accessed | tf_op | source)
XLA Modules:
  0.0 170.6 jit_solution(5783442918940487820)
XLA Ops:
  1.9 1.3 copy.9.live
  3.3 1.4 reshape.7.onsite
  4.7 153.6 %filter_and_project.1 = (f32[256,128]{1,0:T(8,128)}, f32[256,256]{1,0:T(8,128)}, f32[256,256]{1,0:T(8,128)}) custom-call(bf16[16,16,4096]{2,1,0:T(8,128)(2,1)} %hblocks.1, s32[16,16]{1,0:T(8,128)} %cols.1, s32[16,1]{1,0:T(8,128)} %copy.9.live, f32[128,256]{1,0:T(8,128)} %y0.1, bf16[2,64,64]{2,1,0:T(8,128)(2,1)} %reshape.7.onsite, f32[1]{0:T(128)S(6)} %copy.10.low, ...), custom_call_target="tpu_custom_call" | custom-call | tf_op jit(solution)/shard_map/filter_and_project/pallas_call | solution.py:466
  158.3 12.3 %orthonormalize.1 = (f32[128,256]{1,0:T(8,128)}, f32[256,256]{1,0:T(8,128)}) custom-call(f32[256,128]{1,0:T(8,128)} %get-tuple-element.5.cur, f32[256,256]{1,0:T(8,128)} %get-tuple-element.6.gram, f32[256,256]{1,0:T(8,128)} %get-tuple-element.7.half), custom_call_target="tpu_custom_call" | custom-call | tf_op jit(solution)/shard_map/orthonormalize/pallas_call | solution.py:512

commit v4 on v0

v4 whole, which is shorter than its diff:
```python
import jax
import jax.numpy as jnp
from jax import lax
from jax.experimental import pallas as pl
from jax.experimental.pallas import tpu as pltpu
from jax.sharding import PartitionSpec as P

BS = 64
K = 256
PB = 2
DEG = 3
LR = PB * BS
MESH = pl.DeviceIdType.MESH
F32 = jnp.float32
BF16 = jnp.bfloat16

NR = 16
NC = 8
SLAB = K // NR
HALF = 2
KH = K // HALF
CB = 64
STEP = 8
HIGH = lax.Precision.HIGHEST


def rcopy(src, dst, ssem, rsem, dev):
    return pltpu.make_async_remote_copy(
        src_ref=src, dst_ref=dst, send_sem=ssem, recv_sem=rsem, device_id=dev, device_id_type=MESH
    )


def product(a, b, left, right):
    return lax.dot_general(a, b, (((left,), (right,)), ((), ())), preferred_element_type=F32)


def build(blocks, cols, live, pick, tile):
    slots = lax.broadcasted_iota(jnp.int32, cols.shape, 1)
    wanted = jnp.where(slots < live[...], cols[...], -9).astype(F32).astype(BF16)
    count = cols.shape[1]
    depth = 4 * 8 * count
    lane = lax.broadcasted_iota(jnp.int32, (count, depth), 1)
    row = lax.broadcasted_iota(jnp.int32, (count, depth), 0)
    spread = jnp.where(lax.rem(lane, count) == row, 1.0, 0.0).astype(BF16)
    column = product(wanted, spread, 1, 0)
    column = column - lax.rem(lane // (8 * count), 2).astype(F32)

    high = lax.broadcasted_iota(jnp.int32, pick.shape, 0)
    deep = lax.broadcasted_iota(jnp.int32, pick.shape, 1)
    match = lax.rem(high, 16) == 2 * lax.rem(deep // count, 8) + deep // (16 * count)
    pick[...] = jnp.where(match, 2 * (high // 16), -99).astype(F32)
    first = lax.broadcasted_iota(jnp.int32, (8 * count, 2 * BS), 1) < BS
    none = jnp.zeros((8 * count, 2 * BS), BF16)
    return column, first, none


def build_row(i, blocks, column_ref, pick, first, none, tile):
    place = jnp.where(pick[...] == column_ref[pl.ds(i, 1), :], 1.0, 0.0).astype(BF16)
    for half in range(2):
        sides = []
        for p in (2 * half, 2 * half + 1):
            at = [(p * 8 + m) * 2 * BS for m in range(8)]
            plain = jnp.concatenate([blocks[i, :, a : a + 2 * BS] for a in at], axis=0)
            swapped = jnp.concatenate([plain[:, BS:], plain[:, :BS]], axis=1)
            sides.append(
                jnp.concatenate(
                    [
                        jnp.where(first, plain, none),
                        jnp.where(first, none, swapped),
                        jnp.where(first, swapped, none),
                        jnp.where(first, none, plain),
                    ],
                    axis=0,
                )
            )
        rows = product(place, jnp.concatenate(sides, axis=1), 1, 0).astype(BF16)
        for p in range(2):
            at = pl.multiple_of(i * BS + (2 * half + p) * 16, 16)
            for g in range(NR):
                tile[pl.ds(at, 16), g * LR : (g + 1) * LR] = rows[
                    g * 16 : (g + 1) * 16, p * LR : (p + 1) * LR
                ]


def dot_f32(a, b, left, right):
    return lax.dot_general(a, b, (((left,), (right,)), ((), ())), precision=HIGH, preferred_element_type=F32)


def dot_nn(a, b):
    return dot_f32(a, b, 1, 0)


def dot_nt(a, b):
    return dot_f32(a, b, 1, 1)


def dot_tn(a, b):
    return dot_f32(a, b, 0, 0)


def inverse_factor(block):
    rows = lax.broadcasted_iota(jnp.int32, (CB, 2 * CB), 0)
    lanes = lax.broadcasted_iota(jnp.int32, (CB, 2 * CB), 1)
    unit = jnp.where(lanes == rows + CB, 1.0, 0.0).astype(F32)
    x = jnp.where(lanes < CB, jnp.concatenate([block, block], axis=1), unit)
    for s in range(0, CB, STEP):
        col = [jnp.broadcast_to(x[:, s + j : s + j + 1], (CB, 2 * CB)) for j in range(STEP)]
        row = [x[s + j : s + j + 1, :] for j in range(STEP)]
        for j in range(STEP):
            d = col[j][s + j : s + j + 1, :]
            q = lax.rsqrt(d)
            col[j] = col[j] * q
            row[j] = row[j] * q
            for m in range(j + 1, STEP):
                f = col[j][s + m : s + m + 1, :]
                col[m] = col[m] - col[j] * f
                row[m] = row[m] - row[j] * f
        change = col[0] * row[0]
        for j in range(1, STEP):
            change = change + col[j] * row[j]
        x = jnp.where(rows >= s + STEP, x - change, x)
        for j in range(STEP):
            x = jnp.where(rows == s + j, row[j], x)
    return x[:, CB:]


def eliminate(a, b, block):
    k = block * CB
    e = k + CB
    inv = inverse_factor(a[k:e, k:e])
    if k:
        b[k:e, :k] = dot_nn(inv, b[k:e, :k])
    b[k:e, k:e] = inv
    if e < K:
        u = dot_nn(inv, a[k:e, e:])
        a[e:, e:] = a[e:, e:] - dot_tn(u, u)
        b[e:, :e] = b[e:, :e] - dot_tn(u, b[k:e, :e])


def kernel(
    hblocks, cols, live, y0, onsite, low, top, orb_out, proj_out,
    tile, blocks, pick, column, diag,
    vc, vr, ms, sr, mx, xr, zs, zr, ys, yr, ls, lr, prev, cur, part, a1, s2, a2, total, factor, inverse,
    ag_s, ag_r, rs_s, rs_r, ar_s, ar_r, load,
):
    fetch = pltpu.make_async_copy(hblocks, blocks, load)
    fetch.start()
    r = lax.axis_index("row")
    c = lax.axis_index("col")
    core = lax.rem(r, 2)
    x = lax.rem(r // 2, 4)
    yh = r // 8
    z = c // 2
    yl = lax.rem(c, 2)
    sib_r = r + 1 - 2 * core
    yhp_r = lax.rem(r + 8, NR)
    ylp_c = c + 1 - 2 * yl
    sib = (sib_r, c)
    yhp = (yhp_r, c)
    ylp = (r, ylp_c)

    def xrow(d, h=None, k=None):
        return (yh if h is None else h) * 8 + lax.rem(x + d + 4, 4) * 2 + (core if k is None else k)

    def zcol(d, l=None):
        return lax.rem(z + d + 4, 4) * 2 + (yl if l is None else l)

    def part_of(buf, t, u, slot):
        return buf.at[t, u, :, pl.ds(pl.multiple_of(slot * LR, LR), LR)]

    barrier = pltpu.get_barrier_semaphore()

    def greet_row(j, carry):
        pl.semaphore_signal(barrier, inc=1, device_id=(lax.rem(r + j, NR), c), device_id_type=MESH)
        return carry

    def greet_col(j, carry):
        pl.semaphore_signal(barrier, inc=1, device_id=(r, lax.rem(c + j, NC)), device_id_type=MESH)
        return carry

    lax.fori_loop(1, NR, greet_row, 0)
    lax.fori_loop(1, NC, greet_col, 0)

    cur[...] = y0[...].T
    prev[...] = jnp.zeros_like(prev)
    diag[...] = jnp.zeros_like(diag)
    for p in range(PB):
        diag[p * BS : (p + 1) * BS, p * BS : (p + 1) * BS] = onsite[p]
    pl.semaphore_wait(barrier, NR - 1 + NC - 1)


    def send_block(buf, t, u, slot, dev, k):
        side = 0 if buf is vc else 1
        rcopy(
            part_of(buf, t, u, slot), part_of(buf, t, u, slot),
            ag_s.at[t, u, side], ag_r.at[t, u, k], dev,
        ).start()

    def arrived(buf, t, u, slot, k):
        rcopy(
            part_of(buf, t, u, slot), part_of(buf, t, u, slot),
            ag_s.at[t, u, 0], ag_r.at[t, u, k], sib,
        ).wait_recv()

    def blocks_of(buf, t, u, count):
        return buf.at[t, u, :, pl.ds(0, count * LR)]

    def begin(t, u, value):
        vc[t, u, :, pl.ds(pl.multiple_of(r * LR, LR), LR)] = value
        vr[t, u, :, pl.ds(pl.multiple_of(c * LR, LR), LR)] = value
        send_block(vr, t, u, c, ylp, 5)
        send_block(vc, t, u, r, yhp, 1)
        for d in (2, 1, 3):
            send_block(vc, t, u, r, (xrow(d), c), 1 + d)
            send_block(vr, t, u, c, (r, zcol(d)), 6)
        send_block(vc, t, u, r, sib, 0)

    def relay(t, u):
        arrived(vr, t, u, ylp_c, 5)
        for d in (2, 1, 3):
            send_block(vr, t, u, ylp_c, (r, zcol(d)), 6)
        arrived(vc, t, u, yhp_r, 1)
        for d in (2, 1, 3):
            send_block(vc, t, u, yhp_r, (xrow(d), c), 6 + d)
        send_block(vc, t, u, yhp_r, sib, 0)

    def pass_on(t, u):
        for d in (1, 3, 2):
            arrived(vc, t, u, xrow(-d), 1 + d)
            send_block(vc, t, u, xrow(-d), sib, 0)
        for d in (1, 3, 2):
            arrived(vc, t, u, xrow(-d, h=1 - yh), 6 + d)
            send_block(vc, t, u, xrow(-d, h=1 - yh), sib, 0)
        six = blocks_of(vr, t, u, 6)
        rcopy(six, six, ag_s.at[t, u, 1], ag_r.at[t, u, 6], sib).wait_recv()

    def gathered(t, u):
        eight = blocks_of(vc, t, u, 8)
        rcopy(eight, eight, ag_s.at[t, u, 0], ag_r.at[t, u, 0], sib).wait_recv()

    def settle_gather(t, u):
        sent = blocks_of(vc, t, u, 15)
        rcopy(sent, sent, ag_s.at[t, u, 0], ag_r.at[t, u, 0], sib).wait_send()
        sent = blocks_of(vr, t, u, 7)
        rcopy(sent, sent, ag_s.at[t, u, 1], ag_r.at[t, u, 0], sib).wait_send()

    centre = 0.5 * (top[0] + low[0])
    halfwidth = 0.5 * (top[0] - low[0])

    def to_sib(t, u, d):
        return rcopy(
            ms.at[t, u, d, 1 - core], sr.at[t, u, d], rs_s.at[t, u, 0], rs_r.at[t, u, d], sib
        )

    def along_x(t, u, d):
        return rcopy(
            mx.at[t, u, d], xr.at[t, u, d - 1], rs_s.at[t, u, 1], rs_r.at[t, u, 4], (xrow(d), c)
        )

    def along_z(t, u, d):
        return rcopy(
            zs.at[t, u, d], zr.at[t, u, d - 1], rs_s.at[t, u, 2], rs_r.at[t, u, 5], (r, zcol(d))
        )

    def along_y(t, u):
        return (
            rcopy(ys.at[t, u], yr.at[t, u], rs_s.at[t, u, 3], rs_r.at[t, u, 6], yhp),
            rcopy(ls.at[t, u], lr.at[t, u], rs_s.at[t, u, 4], rs_r.at[t, u, 7], ylp),
        )

    def settle_reduce(t, u):
        rcopy(mx.at[t, u], mx.at[t, u], rs_s.at[t, u, 0], rs_r.at[t, u, 0], sib).wait_send()
        rcopy(xr.at[t, u], xr.at[t, u], rs_s.at[t, u, 1], rs_r.at[t, u, 4], sib).wait_send()
        rcopy(zr.at[t, u], zr.at[t, u], rs_s.at[t, u, 2], rs_r.at[t, u, 5], sib).wait_send()
        for cp in along_y(t, u):
            cp.wait_send()

    def products(t, u):
        def mirror(d):
            for h in range(2):
                at = pl.multiple_of(xrow(d, h=h, k=0) * LR, 2 * LR)
                both = product(vr[t, u], tile[:, pl.ds(at, 2 * LR)], 1, 0)
                ms[t, u, d, 0, h] = both[:, :LR]
                ms[t, u, d, 1, h] = both[:, LR:]
            to_sib(t, u, d).start()

        def mirror_on(d):
            to_sib(t, u, d).wait_recv()
            mx[t, u, d] = sr[t, u, d] + ms[t, u, d, core]
            if d:
                along_x(t, u, d).start()

        def direct(d):
            at = pl.multiple_of(zcol(d, l=0) * LR, 2 * LR)
            both = product(vc[t, u], tile[pl.ds(at, 2 * LR), :], 1, 1)
            zs[t, u, d, 0] = both[:, :LR]
            zs[t, u, d, 1] = both[:, LR:]
            if d:
                along_z(t, u, d).start()

        mirror(2)
        mirror(1)
        gathered(t, u)
        mirror_on(2)
        direct(2)
        mirror_on(1)
        mirror(3)
        direct(1)
        mirror_on(3)
        direct(3)
        mirror(0)
        direct(0)
        mirror_on(0)

    def summed(own, got, t, u, at):
        return (own[t, u, 0, at] + got[t, u, 0, at]) + (got[t, u, 1, at] + got[t, u, 2, at])

    def reduce(t, u):
        cp_y, cp_l = along_y(t, u)
        rcopy(xr.at[t, u], xr.at[t, u], rs_s.at[t, u, 1], rs_r.at[t, u, 4], sib).wait_recv()
        ys[t, u] = summed(mx, xr, t, u, 1 - yh)
        cp_y.start()
        rcopy(zr.at[t, u], zr.at[t, u], rs_s.at[t, u, 2], rs_r.at[t, u, 5], sib).wait_recv()
        ls[t, u] = summed(zs, zr, t, u, 1 - yl)
        cp_l.start()

    def update(t, u):
        span = slice(u * KH, (u + 1) * KH)
        cp_y, cp_l = along_y(t, u)
        now = cur[span, :]
        own = product(now.astype(BF16), diag[...], 1, 1)
        own += summed(mx, xr, t, u, yh)
        own += summed(zs, zr, t, u, yl)
        cp_y.wait_recv()
        own += yr[t, u]
        cp_l.wait_recv()
        own += lr[t, u]
        scale = jnp.where(t == 0, 1.0, 2.0).astype(F32)
        following = scale * (own - centre * now) / halfwidth - prev[span, :]
        prev[span, :] = now
        cur[span, :] = following
        begin(t + 1, u, following.astype(BF16))

    for u in range(HALF):
        begin(0, u, cur[u * KH : (u + 1) * KH, :].astype(BF16))

    def degree(t, carry):
        for u in range(HALF):
            relay(t, u)

        @pl.when(t == 0)
        def _():
            fetch.wait()
            spread, first, none = build(blocks, cols, live, pick, tile)
            column[...] = spread

            def one(i, inner):
                build_row(i, blocks, column, pick, first, none, tile)
                return inner

            lax.fori_loop(0, hblocks.shape[0], one, 0)

        @pl.when(t > 0)
        def _():
            for u in range(HALF):
                settle_gather(t - 1, u)
                settle_reduce(t - 1, u)

        for u in range(HALF):
            pass_on(t, u)
        for u in range(HALF):
            products(t, u)
        for u in range(HALF):
            reduce(t, u)
        for u in range(HALF):
            update(t, u)
        return carry

    lax.fori_loop(0, DEG, degree, 0)

    mine = pl.multiple_of(r * SLAB, SLAB)

    def to_row(k):
        def step(j, carry):
            slab = pl.multiple_of(lax.rem(r + j, NR) * SLAB, SLAB)
            rcopy(
                part.at[k, pl.ds(slab, SLAB)], a1.at[k, j - 1], ar_s.at[k, 0], ar_r.at[k, 0],
                (lax.rem(r + j, NR), c),
            ).start()
            return carry

        lax.fori_loop(1, NR, step, 0)

    def to_col(k):
        rcopy(a1.at[k], a1.at[k], ar_s.at[k, 0], ar_r.at[k, 0], sib).wait_recv()
        slab = part[k, pl.ds(mine, SLAB), :]
        for j in range(NR - 1):
            slab = slab + a1[k, j]
        a2[k, c] = slab
        s2[k] = slab

        def step(j, carry):
            rcopy(
                s2.at[k], a2.at[k, c], ar_s.at[k, 1], ar_r.at[k, 1], (r, lax.rem(c + j, NC))
            ).start()
            return carry

        lax.fori_loop(1, NC, step, 0)

    def spread_out(k):
        seven = a2.at[k, pl.ds(0, NC - 1)]
        rcopy(seven, seven, ar_s.at[k, 1], ar_r.at[k, 1], sib).wait_recv()
        slab = a2[k, 0]
        for j in range(1, NC):
            slab = slab + a2[k, j]
        total[k, pl.ds(mine, SLAB), :] = slab

        def step(j, carry):
            here = total.at[k, pl.ds(mine, SLAB)]
            rcopy(here, here, ar_s.at[k, 2], ar_r.at[k, 2], (lax.rem(r + j, NR), c)).start()
            return carry

        lax.fori_loop(1, NR, step, 0)

    def others(k):
        return total.at[k, pl.ds(0, K - SLAB)]

    def collect(k):
        rcopy(others(k), others(k), ar_s.at[k, 2], ar_r.at[k, 2], sib).wait_recv()

    def settle(k):
        rcopy(a1.at[k], a1.at[k], ar_s.at[k, 0], ar_r.at[k, 0], sib).wait_send()
        seven = a2.at[k, pl.ds(0, NC - 1)]
        rcopy(seven, seven, ar_s.at[k, 1], ar_r.at[k, 1], sib).wait_send()
        rcopy(others(k), others(k), ar_s.at[k, 2], ar_r.at[k, 2], sib).wait_send()

    def three(rows, image):
        high = image.astype(BF16)
        rest = image - high.astype(F32)
        mid = rest.astype(BF16)
        low_part = (rest - mid.astype(F32)).astype(BF16)
        return product(rows, high, 1, 1) + (product(rows, mid, 1, 1) + product(rows, low_part, 1, 1))

    rounded = cur[...].astype(BF16)
    part[0] = product(rounded, rounded, 1, 1)
    to_row(0)
    for u in range(HALF):
        relay(DEG, u)
    for u in range(HALF):
        pass_on(DEG, u)
    to_col(0)
    part[1] = three(rounded, 0.5 * product(rounded, diag[...], 1, 1))
    for u in range(HALF):
        gathered(DEG, u)
    for i in range(NC // 2):
        span = slice(i * 2 * LR, (i + 1) * 2 * LR)
        every = vc[DEG].reshape(K, NR * LR)
        image = product(every, tile[span, :], 1, 1)
        part[1] += three(vr[DEG, :, :, span].reshape(K, 2 * LR), image)
        if i == 1:
            spread_out(0)
    to_row(1)
    for u in range(HALF):
        settle_gather(DEG - 1, u)
        settle_reduce(DEG - 1, u)
        settle_gather(DEG, u)
    collect(0)
    scale = 1.0 / (NR * NC * LR)
    factor[...] = total[0] * scale
    inverse[...] = jnp.zeros_like(inverse)
    eliminate(factor, inverse, 0)
    eliminate(factor, inverse, 1)
    to_col(1)
    eliminate(factor, inverse, 2)
    spread_out(1)
    eliminate(factor, inverse, 3)
    w = inverse[...]
    orb_out[...] = dot_f32(cur[...], w, 0, 1)
    settle(0)
    collect(1)
    both = total[1] * scale
    proj_out[...] = dot_nt(dot_nn(w, both) + dot_nt(w, both), w)
    settle(1)


def local(orbitals_in, hblocks, block_cols, live_counts, onsite, cut_low, top_bound):
    vmem = pl.BlockSpec(memory_space=pltpu.VMEM)
    smem = pl.BlockSpec(memory_space=pltpu.SMEM)
    block = (KH, LR)
    steps = (DEG, HALF)
    dma = pltpu.SemaphoreType.DMA
    return pl.pallas_call(
        kernel,
        out_shape=(jax.ShapeDtypeStruct((LR, K), F32), jax.ShapeDtypeStruct((K, K), F32)),
        in_specs=[pl.BlockSpec(memory_space=pl.ANY), vmem, vmem, vmem, vmem, smem, smem],
        out_specs=(vmem, vmem),
        scratch_shapes=[
            pltpu.VMEM((NC * LR, NR * LR), BF16),
            pltpu.VMEM(hblocks.shape, BF16),
            pltpu.VMEM((NR * 16, 32 * hblocks.shape[1]), F32),
            pltpu.VMEM((hblocks.shape[0], 32 * hblocks.shape[1]), F32),
            pltpu.VMEM((LR, LR), BF16),
            pltpu.VMEM((DEG + 1, HALF, KH, NR * LR), BF16),
            pltpu.VMEM((DEG + 1, HALF, KH, NC * LR), BF16),
            pltpu.VMEM(steps + (4, 2, 2) + block, F32),
            pltpu.VMEM(steps + (4, 2) + block, F32),
            pltpu.VMEM(steps + (4, 2) + block, F32),
            pltpu.VMEM(steps + (3, 2) + block, F32),
            pltpu.VMEM(steps + (4, 2) + block, F32),
            pltpu.VMEM(steps + (3, 2) + block, F32),
            pltpu.VMEM(steps + block, F32),
            pltpu.VMEM(steps + block, F32),
            pltpu.VMEM(steps + block, F32),
            pltpu.VMEM(steps + block, F32),
            pltpu.VMEM((K, LR), F32),
            pltpu.VMEM((K, LR), F32),
            pltpu.VMEM((2, K, K), F32),
            pltpu.VMEM((2, NR - 1, SLAB, K), F32),
            pltpu.VMEM((2, SLAB, K), F32),
            pltpu.VMEM((2, NC, SLAB, K), F32),
            pltpu.VMEM((2, K, K), F32),
            pltpu.VMEM((K, K), F32),
            pltpu.VMEM((K, K), F32),
            dma((DEG + 1, HALF, 2)),
            dma((DEG + 1, HALF, 10)),
            dma((DEG, HALF, 5)),
            dma((DEG, HALF, 8)),
            dma((2, 3)),
            dma((2, 3)),
            dma,
        ],
        compiler_params=pltpu.CompilerParams(
            collective_id=0, has_side_effects=True, vmem_limit_bytes=62 * 1024 * 1024
        ),
        name="filter_and_project",
    )(hblocks, block_cols, live_counts, orbitals_in, onsite.reshape(PB, BS, BS), cut_low, top_bound)


def solution(mesh):
    placed = (
        P(("row", "col"), None),
        P("row", "col", None),
        P("row", "col"),
        P("row", "col"),
        P(("row", "col"), None),
        P(),
        P(),
    )
    return jax.shard_map(
        local, mesh=mesh, in_specs=placed, out_specs=(P(("row", "col"), None), P()), check_vma=False
    )
```

time: 904 us -> 146 us (0.16)
  waiting for transfers between devices: 641 us -> 0 us
  Pallas kernels: 0 us -> 138 us
  blocking collectives: 102 us -> 0 us
  other arithmetic: 64.7 us -> 0 us
  matrix products: 52.9 us -> 0 us
  local copies, waits for them, and re-layouts: 25.5 us -> 5.99 us
  between operations: 16.8 us -> 1.93 us
    reduce_scatter x8 -> x0, waiting for transfers between devices: 424 us -> none  [the longest x4 265 us: apply(): lax.psum_scatter(mirror_rows(dense_tile, lax.all_gather(rounded, 'col', a...]
    psum x1 -> x0, waiting for transfers between devices: 153 us -> none  [local(): gram_total, cross_total = lax.psum((gram_part, cross_part), ('row', 'col'))]
    pallas_call x0 -> x1, Pallas kernels: none -> 138 us  [local(): pl.pallas_call(kernel, out_shape=(jax.ShapeDtypeStruct((LR, K), F32), jax...]
    all_gather x4 -> x0, blocking collectives: 102 us -> none  [apply(): lax.all_gather(rounded, 'col', axis=0, tiled=True)]
    all_gather x4 -> x0, waiting for transfers between devices: 64.1 us -> none  [apply(): lax.all_gather(rounded, 'row', axis=0, tiled=True)]
    another operation x11 -> x0, other arithmetic: 55.1 us -> none  [the longest x7 34.7 us: local(): factor = jnp.linalg.cholesky(gram_matrix)]
    dot_general x15 -> x0, matrix products: 49.7 us -> none  [the longest x4 19.4 us: mirror_rows(): lax.dot_general(dense_tile, row_set, (((0,), (0,)), ((), ())), preferred_...]
    reshape x3 -> x1, local copies, waits for them, and re-layouts: 19.4 us -> 1.43 us  [local(): onsite.reshape(PB, BS, BS)]
  transfers between devices with their start and end apart: 13 -> 0, of which waited for: 12 -> 0; matrix products, arithmetic and copies ran while one was open for 8% -> 0% of each run, Pallas kernels for 0% -> 0%
where the time goes in v4:
time: 146 us
  Pallas kernels  138 us (95%)
  local copies, waits for them, and re-layouts  5.99 us (4%)
  between operations  1.93 us (1%)
    pallas_call x1, Pallas kernels, local(): pl.pallas_call(kernel, out_shape=(jax.ShapeDtypeStruct((LR, K), F32), jax...  138 us
    unnamed x3, local copies, waits for them, and re-layouts  4.57 us

profile of v4, /device:TPU:1, one launch (start us, length us, event | category | flops | bytes accessed | tf_op | source)
XLA Modules:
  0.0 146.2 jit_solution(11582722480019312415)
XLA Ops:
  1.9 1.3 copy.9.live
  3.3 1.4 reshape.7.onsite
  4.7 138.3 %filter_and_project.1 = (f32[128,256]{1,0:T(8,128)}, f32[256,256]{1,0:T(8,128)}) custom-call(bf16[16,16,4096]{2,1,0:T(8,128)(2,1)} %hblocks.1, s32[16,16]{1,0:T(8,128)} %cols.1, s32[16,1]{1,0:T(8,128)} %copy.9.live, f32[128,256]{1,0:T(8,128)} %y0.1, bf16[2,64,64]{2,1,0:T(8,128)(2,1)} %reshape.7.onsite, f32[1]{0:T(128)S(6)} %copy.12.low, f32[1]{0:T(128)S(6)} %copy.13.top), custom_call_target="tpu_custom_call" | custom-call | tf_op jit(solution)/shard_map/filter_and_project/pallas_call | solution.py:492
  143.0 1.6 %copy.14 = f32[128,256]{1,0:T(8,128)} copy(f32[128,256]{1,0:T(8,128)} %get-tuple-element.4) | data formatting | bytes 262144
  144.6 1.7 %copy.15 = f32[256,256]{1,0:T(8,128)} copy(f32[256,256]{1,0:T(8,128)} %get-tuple-element.5) | data formatting | bytes 524288

commit v5 on v4

--- a/solution.py
+++ b/solution.py
@@ -17,7 +17,7 @@
 NR = 16
 NC = 8
 SLAB = K // NR
-HALF = 2
+HALF = 1
 KH = K // HALF
 CB = 64
 STEP = 8
@@ -36,7 +36,9 @@
 
 def build(blocks, cols, live, pick, tile):
     slots = lax.broadcasted_iota(jnp.int32, cols.shape, 1)
-    wanted = jnp.where(slots < live[...], cols[...], -9).astype(F32).astype(BF16)
+    same = lax.broadcasted_iota(jnp.int32, cols.shape, 0) == slots
+    counts = jnp.where(same, live[...].astype(F32), 0.0).sum(axis=1, keepdims=True)
+    wanted = jnp.where(slots.astype(F32) < counts, cols[...].astype(F32), -9.0).astype(BF16)
     count = cols.shape[1]
     depth = 4 * 8 * count
     lane = lax.broadcasted_iota(jnp.int32, (count, depth), 1)
@@ -52,6 +54,24 @@
     first = lax.broadcasted_iota(jnp.int32, (8 * count, 2 * BS), 1) < BS
     none = jnp.zeros((8 * count, 2 * BS), BF16)
     return column, first, none
+
+
+def build_diag(onsite, diag):
+    tiles = onsite[...].astype(F32)
+    stack = jnp.concatenate(
+        [tiles[:, m * 2 * BS : (m + 1) * 2 * BS] for m in range(BS // 2)], axis=0
+    ).astype(BF16)
+    row = lax.broadcasted_iota(jnp.int32, (BS, BS), 0)
+    deep = lax.broadcasted_iota(jnp.int32, (BS, BS), 1)
+    even = lax.rem(lax.broadcasted_iota(jnp.int32, (BS, 2 * BS), 0), 2) == 0
+    left = lax.broadcasted_iota(jnp.int32, (BS, 2 * BS), 1) < BS
+    for p in range(PB):
+        pick = jnp.where(deep == row // 2 * PB + p, 1.0, 0.0).astype(BF16)
+        plain = product(pick, stack, 1, 0)
+        swapped = jnp.concatenate([plain[:, BS:], plain[:, :BS]], axis=1)
+        rows = jnp.where(even, plain, swapped) if p == 0 else jnp.where(even, swapped, plain)
+        rows = jnp.where(left, rows, 0.0) if p == 0 else jnp.where(left, 0.0, rows)
+        diag[p * BS : (p + 1) * BS, :] = rows.astype(BF16)
 
 
 def build_row(i, blocks, column_ref, pick, first, none, tile):
@@ -138,7 +158,7 @@
 
 
 def kernel(
-    hblocks, cols, live, y0, onsite, low, top, orb_out, proj_out,
+    hblocks, cols, live, y0, onsite, low, top, orb_out, inv_out, ritz_out,
     tile, blocks, pick, column, diag,
     vc, vr, ms, sr, mx, xr, zs, zr, ys, yr, ls, lr, prev, cur, part, a1, s2, a2, total, factor, inverse,
     ag_s, ag_r, rs_s, rs_r, ar_s, ar_r, load,
@@ -183,9 +203,17 @@
 
     cur[...] = y0[...].T
     prev[...] = jnp.zeros_like(prev)
-    diag[...] = jnp.zeros_like(diag)
-    for p in range(PB):
-        diag[p * BS : (p + 1) * BS, p * BS : (p + 1) * BS] = onsite[p]
+    build_diag(onsite, diag)
+    fetch.wait()
+    spread, first, none = build(blocks, cols, live, pick, tile)
+    column[...] = spread
+
+    def one(i, carry):
+        build_row(i, blocks, column, pick, first, none, tile)
+        return carry
+
+    early = hblocks.shape[0] // 2
+    lax.fori_loop(0, early, one, 0)
     pl.semaphore_wait(barrier, NR - 1 + NC - 1)
 
 
@@ -244,28 +272,32 @@
         sent = blocks_of(vr, t, u, 7)
         rcopy(sent, sent, ag_s.at[t, u, 1], ag_r.at[t, u, 0], sib).wait_send()
 
-    centre = 0.5 * (top[0] + low[0])
-    halfwidth = 0.5 * (top[0] - low[0])
-
-    def to_sib(t, u, d):
+    centre = 0.5 * (top[...] + low[...])
+    halfwidth = 0.5 * (top[...] - low[...])
+
+
+    def to_sib(t, u, e, d):
         return rcopy(
-            ms.at[t, u, d, 1 - core], sr.at[t, u, d], rs_s.at[t, u, 0], rs_r.at[t, u, d], sib
+            ms.at[t, u, e, d, 1 - core], sr.at[t, u, e, d],
+            rs_s.at[t, u, 0], rs_r.at[t, u, e * 4 + d], sib,
         )
 
-    def along_x(t, u, d):
+    def along_x(t, u, e, d):
         return rcopy(
-            mx.at[t, u, d], xr.at[t, u, d - 1], rs_s.at[t, u, 1], rs_r.at[t, u, 4], (xrow(d), c)
+            mx.at[t, u, e, d], xr.at[t, u, e, d - 1],
+            rs_s.at[t, u, 1], rs_r.at[t, u, 8 + e], (xrow(d), c),
         )
 
-    def along_z(t, u, d):
+    def along_z(t, u, e, d):
         return rcopy(
-            zs.at[t, u, d], zr.at[t, u, d - 1], rs_s.at[t, u, 2], rs_r.at[t, u, 5], (r, zcol(d))
+            zs.at[t, u, e, d], zr.at[t, u, e, d - 1],
+            rs_s.at[t, u, 2], rs_r.at[t, u, 10 + e], (r, zcol(d)),
         )
 
     def along_y(t, u):
         return (
-            rcopy(ys.at[t, u], yr.at[t, u], rs_s.at[t, u, 3], rs_r.at[t, u, 6], yhp),
-            rcopy(ls.at[t, u], lr.at[t, u], rs_s.at[t, u, 4], rs_r.at[t, u, 7], ylp),
+            rcopy(ys.at[t, u], yr.at[t, u], rs_s.at[t, u, 3], rs_r.at[t, u, 12], yhp),
+            rcopy(ls.at[t, u], lr.at[t, u], rs_s.at[t, u, 4], rs_r.at[t, u, 13], ylp),
         )
 
     def settle_reduce(t, u):
@@ -275,36 +307,37 @@
         for cp in along_y(t, u):
             cp.wait_send()
 
-    def products(t, u):
+    def products(t, u, e):
         def mirror(d):
-            for h in range(2):
-                at = pl.multiple_of(xrow(d, h=h, k=0) * LR, 2 * LR)
-                both = product(vr[t, u], tile[:, pl.ds(at, 2 * LR)], 1, 0)
-                ms[t, u, d, 0, h] = both[:, :LR]
-                ms[t, u, d, 1, h] = both[:, LR:]
-            to_sib(t, u, d).start()
+            at = pl.multiple_of(xrow(d, h=yh if e == 0 else 1 - yh, k=0) * LR, 2 * LR)
+            both = product(vr[t, u], tile[:, pl.ds(at, 2 * LR)], 1, 0)
+            ms[t, u, e, d, 0] = both[:, :LR]
+            ms[t, u, e, d, 1] = both[:, LR:]
+            to_sib(t, u, e, d).start()
 
         def mirror_on(d):
-            to_sib(t, u, d).wait_recv()
-            mx[t, u, d] = sr[t, u, d] + ms[t, u, d, core]
+            to_sib(t, u, e, d).wait_recv()
+            mx[t, u, e, d] = sr[t, u, e, d] + ms[t, u, e, d, core]
             if d:
-                along_x(t, u, d).start()
+                along_x(t, u, e, d).start()
 
         def direct(d):
-            at = pl.multiple_of(zcol(d, l=0) * LR, 2 * LR)
-            both = product(vc[t, u], tile[pl.ds(at, 2 * LR), :], 1, 1)
-            zs[t, u, d, 0] = both[:, :LR]
-            zs[t, u, d, 1] = both[:, LR:]
+            if e:
+                at = pl.multiple_of(zcol(d, l=0) * LR, 2 * LR)
+                both = product(vc[t, u], tile[pl.ds(at, 2 * LR), :], 1, 1)
+                zs[t, u, yl, d] = both[:, :LR]
+                zs[t, u, 1 - yl, d] = both[:, LR:]
             if d:
-                along_z(t, u, d).start()
+                along_z(t, u, e, d).start()
 
         mirror(2)
         mirror(1)
-        gathered(t, u)
+        mirror(3)
+        if e:
+            gathered(t, u)
+        direct(2)
         mirror_on(2)
-        direct(2)
         mirror_on(1)
-        mirror(3)
         direct(1)
         mirror_on(3)
         direct(3)
@@ -312,16 +345,24 @@
         direct(0)
         mirror_on(0)
 
-    def summed(own, got, t, u, at):
-        return (own[t, u, 0, at] + got[t, u, 0, at]) + (got[t, u, 1, at] + got[t, u, 2, at])
+    def summed(own, got, t, u, e):
+        return (own[t, u, e, 0] + got[t, u, e, 0]) + (got[t, u, e, 1] + got[t, u, e, 2])
+
+    def arrived_x(t, u, e):
+        all_x = xr.at[t, u, e]
+        rcopy(all_x, all_x, rs_s.at[t, u, 1], rs_r.at[t, u, 8 + e], sib).wait_recv()
+
+    def arrived_z(t, u, e):
+        all_z = zr.at[t, u, e]
+        rcopy(all_z, all_z, rs_s.at[t, u, 2], rs_r.at[t, u, 10 + e], sib).wait_recv()
 
     def reduce(t, u):
         cp_y, cp_l = along_y(t, u)
-        rcopy(xr.at[t, u], xr.at[t, u], rs_s.at[t, u, 1], rs_r.at[t, u, 4], sib).wait_recv()
-        ys[t, u] = summed(mx, xr, t, u, 1 - yh)
+        arrived_x(t, u, 1)
+        ys[t, u] = summed(mx, xr, t, u, 1)
         cp_y.start()
-        rcopy(zr.at[t, u], zr.at[t, u], rs_s.at[t, u, 2], rs_r.at[t, u, 5], sib).wait_recv()
-        ls[t, u] = summed(zs, zr, t, u, 1 - yl)
+        arrived_z(t, u, 1)
+        ls[t, u] = summed(zs, zr, t, u, 1)
         cp_l.start()
 
     def update(t, u):
@@ -329,8 +370,10 @@
         cp_y, cp_l = along_y(t, u)
         now = cur[span, :]
         own = product(now.astype(BF16), diag[...], 1, 1)
-        own += summed(mx, xr, t, u, yh)
-        own += summed(zs, zr, t, u, yl)
+        arrived_x(t, u, 0)
+        own += summed(mx, xr, t, u, 0)
+        arrived_z(t, u, 0)
+        own += summed(zs, zr, t, u, 0)
         cp_y.wait_recv()
         own += yr[t, u]
         cp_l.wait_recv()
@@ -350,15 +393,7 @@
 
         @pl.when(t == 0)
         def _():
-            fetch.wait()
-            spread, first, none = build(blocks, cols, live, pick, tile)
-            column[...] = spread
-
-            def one(i, inner):
-                build_row(i, blocks, column, pick, first, none, tile)
-                return inner
-
-            lax.fori_loop(0, hblocks.shape[0], one, 0)
+            lax.fori_loop(early, hblocks.shape[0], one, 0)
 
         @pl.when(t > 0)
         def _():
@@ -368,8 +403,9 @@
 
         for u in range(HALF):
             pass_on(t, u)
-        for u in range(HALF):
-            products(t, u)
+        for e in (1, 0):
+            for u in range(HALF):
+                products(t, u, e)
         for u in range(HALF):
             reduce(t, u)
         for u in range(HALF):
@@ -457,43 +493,51 @@
         every = vc[DEG].reshape(K, NR * LR)
         image = product(every, tile[span, :], 1, 1)
         part[1] += three(vr[DEG, :, :, span].reshape(K, 2 * LR), image)
-        if i == 1:
-            spread_out(0)
     to_row(1)
+    spread_out(0)
     for u in range(HALF):
         settle_gather(DEG - 1, u)
         settle_reduce(DEG - 1, u)
         settle_gather(DEG, u)
+    scale = 1.0 / (NR * NC * LR)
+    inverse[...] = jnp.zeros_like(inverse)
+    to_col(1)
     collect(0)
-    scale = 1.0 / (NR * NC * LR)
     factor[...] = total[0] * scale
-    inverse[...] = jnp.zeros_like(inverse)
     eliminate(factor, inverse, 0)
     eliminate(factor, inverse, 1)
-    to_col(1)
+    spread_out(1)
     eliminate(factor, inverse, 2)
-    spread_out(1)
     eliminate(factor, inverse, 3)
     w = inverse[...]
+    inv_out[...] = w
     orb_out[...] = dot_f32(cur[...], w, 0, 1)
     settle(0)
     collect(1)
-    both = total[1] * scale
-    proj_out[...] = dot_nt(dot_nn(w, both) + dot_nt(w, both), w)
+    ritz_out[...] = total[1] * scale
     settle(1)
+
+
+def project(made, inverse, half, orb, proj):
+    w = inverse[...]
+    both = half[...]
+    orb[...] = made[...]
+    proj[...] = dot_nt(dot_nn(w, both + both.T), w)
 
 
 def local(orbitals_in, hblocks, block_cols, live_counts, onsite, cut_low, top_bound):
     vmem = pl.BlockSpec(memory_space=pltpu.VMEM)
-    smem = pl.BlockSpec(memory_space=pltpu.SMEM)
+    anywhere = pl.BlockSpec(memory_space=pl.ANY)
     block = (KH, LR)
     steps = (DEG, HALF)
     dma = pltpu.SemaphoreType.DMA
-    return pl.pallas_call(
+    square = jax.ShapeDtypeStruct((K, K), F32)
+    rows = jax.ShapeDtypeStruct((LR, K), F32)
+    orbitals, inverse, half = pl.pallas_call(
         kernel,
-        out_shape=(jax.ShapeDtypeStruct((LR, K), F32), jax.ShapeDtypeStruct((K, K), F32)),
-        in_specs=[pl.BlockSpec(memory_space=pl.ANY), vmem, vmem, vmem, vmem, smem, smem],
-        out_specs=(vmem, vmem),
+        out_shape=(rows, square, square),
+        in_specs=[anywhere] + [vmem] * 6,
+        out_specs=(vmem, vmem, vmem),
         scratch_shapes=[
             pltpu.VMEM((NC * LR, NR * LR), BF16),
             pltpu.VMEM(hblocks.shape, BF16),
@@ -502,12 +546,12 @@
             pltpu.VMEM((LR, LR), BF16),
             pltpu.VMEM((DEG + 1, HALF, KH, NR * LR), BF16),
             pltpu.VMEM((DEG + 1, HALF, KH, NC * LR), BF16),
-            pltpu.VMEM(steps + (4, 2, 2) + block, F32),
-            pltpu.VMEM(steps + (4, 2) + block, F32),
-            pltpu.VMEM(steps + (4, 2) + block, F32),
-            pltpu.VMEM(steps + (3, 2) + block, F32),
-            pltpu.VMEM(steps + (4, 2) + block, F32),
-            pltpu.VMEM(steps + (3, 2) + block, F32),
+            pltpu.VMEM(steps + (2, 4, 2) + block, F32),
+            pltpu.VMEM(steps + (2, 4) + block, F32),
+            pltpu.VMEM(steps + (2, 4) + block, F32),
+            pltpu.VMEM(steps + (2, 3) + block, F32),
+            pltpu.VMEM(steps + (2, 4) + block, F32),
+            pltpu.VMEM(steps + (2, 3) + block, F32),
             pltpu.VMEM(steps + block, F32),
             pltpu.VMEM(steps + block, F32),
             pltpu.VMEM(steps + block, F32),
@@ -524,7 +568,7 @@
             dma((DEG + 1, HALF, 2)),
             dma((DEG + 1, HALF, 10)),
             dma((DEG, HALF, 5)),
-            dma((DEG, HALF, 8)),
+            dma((DEG, HALF, 14)),
             dma((2, 3)),
             dma((2, 3)),
             dma,
@@ -533,7 +577,15 @@
             collective_id=0, has_side_effects=True, vmem_limit_bytes=62 * 1024 * 1024
         ),
         name="filter_and_project",
-    )(hblocks, block_cols, live_counts, orbitals_in, onsite.reshape(PB, BS, BS), cut_low, top_bound)
+    )(
+        hblocks, block_cols, live_counts.reshape(1, -1), orbitals_in, onsite,
+        cut_low, top_bound,
+    )
+    return pl.pallas_call(
+        project,
+        out_shape=(rows, square),
+        name="project",
+    )(orbitals, inverse, half)
 
 
 def solution(mesh):

time: 146 us -> 134 us (0.918)
  Pallas kernels: 138 us -> 132 us
  local copies, waits for them, and re-layouts: 5.99 us -> 0 us
    pallas_call x1 -> x2, Pallas kernels: 138 us -> 132 us  [the longest x1 129 us: local(): pl.pallas_call(kernel, out_shape=(rows, square, square), in_specs=[anywhe...]
    unnamed x3 -> x0, local copies, waits for them, and re-layouts: 4.57 us -> none
where the time goes in v5:
time: 134 us
  Pallas kernels  132 us (99%)
  between operations  1.93 us (1%)
    pallas_call x1, Pallas kernels, local(): pl.pallas_call(kernel, out_shape=(rows, square, square), in_specs=[anywhe...  129 us
    pallas_call x1, Pallas kernels, local(): pl.pallas_call(project, out_shape=(rows, square), name='project')  2.9 us

profile of v5, /device:TPU:1, one launch (start us, length us, event | category | flops | bytes accessed | tf_op | source)
XLA Modules:
  0.0 134.0 jit_solution(14793647086552595354)
XLA Ops:
  1.9 129.2 %filter_and_project.1 = (f32[128,256]{1,0:T(8,128)}, f32[256,256]{1,0:T(8,128)}, f32[256,256]{1,0:T(8,128)}) custom-call(bf16[16,16,4096]{2,1,0:T(8,128)(2,1)} %hblocks.1, s32[16,16]{1,0:T(8,128)} %cols.1, s32[1,16]{1,0:T(1,128)} %bitcast.1, f32[128,256]{1,0:T(8,128)} %y0.1, bf16[2,4096]{1,0:T(2,128)(2,1)} %onsite.1, f32[1]{0:T(128)S(6)} %copy.9.low, ...), custom_call_target="tpu_custom_call" | custom-call | tf_op jit(solution)/shard_map/filter_and_project/pallas_call | solution.py:536
  131.1 2.9 %project.1 = (f32[128,256]{1,0:T(8,128)}, f32[256,256]{1,0:T(8,128)}) custom-call(f32[128,256]{1,0:T(8,128)} %get-tuple-element.5.made, f32[256,256]{1,0:T(8,128)} %get-tuple-element.6.inverse, f32[256,256]{1,0:T(8,128)} %get-tuple-element.7.half), custom_call_target="tpu_custom_call" | custom-call | tf_op jit(solution)/shard_map/project/pallas_call | solution.py:584

commit v6 on v5

--- a/solution.py
+++ b/solution.py
@@ -160,7 +160,7 @@
 def kernel(
     hblocks, cols, live, y0, onsite, low, top, orb_out, inv_out, ritz_out,
     tile, blocks, pick, column, diag,
-    vc, vr, ms, sr, mx, xr, zs, zr, ys, yr, ls, lr, prev, cur, part, a1, s2, a2, total, factor, inverse,
+    vc, vr, ms, sr, mx, xr, zs, zr, ys, yr, ls, lr, zf, prev, cur, part, a1, s2, a2, total, factor, inverse,
     ag_s, ag_r, rs_s, rs_r, ar_s, ar_r, load,
 ):
     fetch = pltpu.make_async_copy(hblocks, blocks, load)
@@ -203,17 +203,6 @@
 
     cur[...] = y0[...].T
     prev[...] = jnp.zeros_like(prev)
-    build_diag(onsite, diag)
-    fetch.wait()
-    spread, first, none = build(blocks, cols, live, pick, tile)
-    column[...] = spread
-
-    def one(i, carry):
-        build_row(i, blocks, column, pick, first, none, tile)
-        return carry
-
-    early = hblocks.shape[0] // 2
-    lax.fori_loop(0, early, one, 0)
     pl.semaphore_wait(barrier, NR - 1 + NC - 1)
 
 
@@ -256,11 +245,13 @@
         for d in (1, 3, 2):
             arrived(vc, t, u, xrow(-d), 1 + d)
             send_block(vc, t, u, xrow(-d), sib, 0)
+        six = blocks_of(vr, t, u, 6)
+        rcopy(six, six, ag_s.at[t, u, 1], ag_r.at[t, u, 6], sib).wait_recv()
+
+    def pass_far(t, u):
         for d in (1, 3, 2):
             arrived(vc, t, u, xrow(-d, h=1 - yh), 6 + d)
             send_block(vc, t, u, xrow(-d, h=1 - yh), sib, 0)
-        six = blocks_of(vr, t, u, 6)
-        rcopy(six, six, ag_s.at[t, u, 1], ag_r.at[t, u, 6], sib).wait_recv()
 
     def gathered(t, u):
         eight = blocks_of(vc, t, u, 8)
@@ -291,7 +282,7 @@
     def along_z(t, u, e, d):
         return rcopy(
             zs.at[t, u, e, d], zr.at[t, u, e, d - 1],
-            rs_s.at[t, u, 2], rs_r.at[t, u, 10 + e], (r, zcol(d)),
+            rs_s.at[t, u, 2 + 3 * e], rs_r.at[t, u, 10 + e], (r, zcol(d)),
         )
 
     def along_y(t, u):
@@ -300,11 +291,16 @@
             rcopy(ls.at[t, u], lr.at[t, u], rs_s.at[t, u, 4], rs_r.at[t, u, 13], ylp),
         )
 
+    def far_z(t, u):
+        return rcopy(zs.at[t, u, 1, 2], zf.at[t, u], rs_s.at[t, u, 6], rs_r.at[t, u, 14], ylp)
+
     def settle_reduce(t, u):
         rcopy(mx.at[t, u], mx.at[t, u], rs_s.at[t, u, 0], rs_r.at[t, u, 0], sib).wait_send()
         rcopy(xr.at[t, u], xr.at[t, u], rs_s.at[t, u, 1], rs_r.at[t, u, 4], sib).wait_send()
-        rcopy(zr.at[t, u], zr.at[t, u], rs_s.at[t, u, 2], rs_r.at[t, u, 5], sib).wait_send()
-        for cp in along_y(t, u):
+        for e in range(2):
+            sent = zr.at[t, u, e, pl.ds(0, 3 - e)]
+            rcopy(sent, sent, rs_s.at[t, u, 2 + 3 * e], rs_r.at[t, u, 5], sib).wait_send()
+        for cp in along_y(t, u) + (far_z(t, u),):
             cp.wait_send()
 
     def products(t, u, e):
@@ -327,23 +323,38 @@
                 both = product(vc[t, u], tile[pl.ds(at, 2 * LR), :], 1, 1)
                 zs[t, u, yl, d] = both[:, :LR]
                 zs[t, u, 1 - yl, d] = both[:, LR:]
-            if d:
+            if d == 2 and e == 0:
+                far_z(t, u).wait_recv()
+                zs[t, u, 0, 2] = zs[t, u, 0, 2] + zf[t, u]
+            if d == 2 and e == 1:
+                far_z(t, u).start()
+            elif d:
                 along_z(t, u, e, d).start()
 
-        mirror(2)
-        mirror(1)
-        mirror(3)
         if e:
+            mirror(2)
+            mirror(1)
+            pass_far(t, u)
+            mirror(3)
+            for d in (2, 1, 3):
+                mirror_on(d)
             gathered(t, u)
-        direct(2)
-        mirror_on(2)
-        mirror_on(1)
-        direct(1)
-        mirror_on(3)
-        direct(3)
-        mirror(0)
-        direct(0)
-        mirror_on(0)
+            for d in (2, 1, 3):
+                direct(d)
+            mirror(0)
+            direct(0)
+            mirror_on(0)
+        else:
+            for d in (1, 3, 2):
+                mirror(d)
+            for d in (1, 3):
+                direct(d)
+                mirror_on(d)
+            mirror_on(2)
+            mirror(0)
+            direct(0)
+            mirror_on(0)
+            direct(2)
 
     def summed(own, got, t, u, e):
         return (own[t, u, e, 0] + got[t, u, e, 0]) + (got[t, u, e, 1] + got[t, u, e, 2])
@@ -353,7 +364,7 @@
         rcopy(all_x, all_x, rs_s.at[t, u, 1], rs_r.at[t, u, 8 + e], sib).wait_recv()
 
     def arrived_z(t, u, e):
-        all_z = zr.at[t, u, e]
+        all_z = zr.at[t, u, e, pl.ds(0, 3 - e)]
         rcopy(all_z, all_z, rs_s.at[t, u, 2], rs_r.at[t, u, 10 + e], sib).wait_recv()
 
     def reduce(t, u):
@@ -362,7 +373,7 @@
         ys[t, u] = summed(mx, xr, t, u, 1)
         cp_y.start()
         arrived_z(t, u, 1)
-        ls[t, u] = summed(zs, zr, t, u, 1)
+        ls[t, u] = (zs[t, u, 1, 0] + zr[t, u, 1, 0]) + zr[t, u, 1, 2]
         cp_l.start()
 
     def update(t, u):
@@ -387,6 +398,18 @@
     for u in range(HALF):
         begin(0, u, cur[u * KH : (u + 1) * KH, :].astype(BF16))
 
+    build_diag(onsite, diag)
+    fetch.wait()
+    spread, first, none = build(blocks, cols, live, pick, tile)
+    column[...] = spread
+
+    def one(i, carry):
+        build_row(i, blocks, column, pick, first, none, tile)
+        return carry
+
+    early = hblocks.shape[0] // 2
+    lax.fori_loop(0, early, one, 0)
+
     def degree(t, carry):
         for u in range(HALF):
             relay(t, u)
@@ -484,6 +507,7 @@
         relay(DEG, u)
     for u in range(HALF):
         pass_on(DEG, u)
+        pass_far(DEG, u)
     to_col(0)
     part[1] = three(rounded, 0.5 * product(rounded, diag[...], 1, 1))
     for u in range(HALF):
@@ -556,6 +580,7 @@
             pltpu.VMEM(steps + block, F32),
             pltpu.VMEM(steps + block, F32),
             pltpu.VMEM(steps + block, F32),
+            pltpu.VMEM(steps + block, F32),
             pltpu.VMEM((K, LR), F32),
             pltpu.VMEM((K, LR), F32),
             pltpu.VMEM((2, K, K), F32),
@@ -567,8 +592,8 @@
             pltpu.VMEM((K, K), F32),
             dma((DEG + 1, HALF, 2)),
             dma((DEG + 1, HALF, 10)),
-            dma((DEG, HALF, 5)),
-            dma((DEG, HALF, 14)),
+            dma((DEG, HALF, 7)),
+            dma((DEG, HALF, 15)),
             dma((2, 3)),
             dma((2, 3)),
             dma,

time: 134 us -> 129 us (0.963)
  Pallas kernels: 132 us -> 127 us
    pallas_call x1, Pallas kernels: 129 us -> 124 us  [local(): pl.pallas_call(kernel, out_shape=(rows, square, square), in_specs=[anywhe...]
where the time goes in v6:
time: 129 us
  Pallas kernels  127 us (98%)
  between operations  1.93 us (1%)
    pallas_call x1, Pallas kernels, local(): pl.pallas_call(kernel, out_shape=(rows, square, square), in_specs=[anywhe...  124 us
    pallas_call x1, Pallas kernels, local(): pl.pallas_call(project, out_shape=(rows, square), name='project')  2.91 us

profile of v6, /device:TPU:1, one launch (start us, length us, event | category | flops | bytes accessed | tf_op | source)
XLA Modules:
  0.0 129.3 jit_solution(11211167106484723114)
XLA Ops:
  1.9 124.4 %filter_and_project.1 = (f32[128,256]{1,0:T(8,128)}, f32[256,256]{1,0:T(8,128)}, f32[256,256]{1,0:T(8,128)}) custom-call(bf16[16,16,4096]{2,1,0:T(8,128)(2,1)} %hblocks.1, s32[16,16]{1,0:T(8,128)} %cols.1, s32[1,16]{1,0:T(1,128)} %bitcast.1, f32[128,256]{1,0:T(8,128)} %y0.1, bf16[2,4096]{1,0:T(2,128)(2,1)} %onsite.1, f32[1]{0:T(128)S(6)} %copy.9.low, ...), custom_call_target="tpu_custom_call" | custom-call | tf_op jit(solution)/shard_map/filter_and_project/pallas_call | solution.py:560
  126.4 2.9 %project.1 = (f32[128,256]{1,0:T(8,128)}, f32[256,256]{1,0:T(8,128)}) custom-call(f32[128,256]{1,0:T(8,128)} %get-tuple-element.5.made, f32[256,256]{1,0:T(8,128)} %get-tuple-element.6.inverse, f32[256,256]{1,0:T(8,128)} %get-tuple-element.7.half), custom_call_target="tpu_custom_call" | custom-call | tf_op jit(solution)/shard_map/project/pallas_call | solution.py:609

commit v7 on v6

--- a/solution.py
+++ b/solution.py
@@ -188,6 +188,9 @@
     def part_of(buf, t, u, slot):
         return buf.at[t, u, :, pl.ds(pl.multiple_of(slot * LR, LR), LR)]
 
+    upper = yh == 0
+    lower = yh == 1
+    yr[...] = jnp.zeros_like(yr)
     barrier = pltpu.get_barrier_semaphore()
 
     def greet_row(j, carry):
@@ -226,7 +229,11 @@
         vc[t, u, :, pl.ds(pl.multiple_of(r * LR, LR), LR)] = value
         vr[t, u, :, pl.ds(pl.multiple_of(c * LR, LR), LR)] = value
         send_block(vr, t, u, c, ylp, 5)
-        send_block(vc, t, u, r, yhp, 1)
+
+        @pl.when(lower)
+        def _():
+            send_block(vc, t, u, r, yhp, 1)
+
         for d in (2, 1, 3):
             send_block(vc, t, u, r, (xrow(d), c), 1 + d)
             send_block(vr, t, u, c, (r, zcol(d)), 6)
@@ -236,10 +243,13 @@
         arrived(vr, t, u, ylp_c, 5)
         for d in (2, 1, 3):
             send_block(vr, t, u, ylp_c, (r, zcol(d)), 6)
-        arrived(vc, t, u, yhp_r, 1)
-        for d in (2, 1, 3):
-            send_block(vc, t, u, yhp_r, (xrow(d), c), 6 + d)
-        send_block(vc, t, u, yhp_r, sib, 0)
+
+        @pl.when(upper)
+        def _():
+            arrived(vc, t, u, yhp_r, 1)
+            for d in (2, 1, 3):
+                send_block(vc, t, u, yhp_r, (xrow(d), c), 6 + d)
+            send_block(vc, t, u, yhp_r, sib, 0)
 
     def pass_on(t, u):
         for d in (1, 3, 2):
@@ -249,19 +259,28 @@
         rcopy(six, six, ag_s.at[t, u, 1], ag_r.at[t, u, 6], sib).wait_recv()
 
     def pass_far(t, u):
-        for d in (1, 3, 2):
-            arrived(vc, t, u, xrow(-d, h=1 - yh), 6 + d)
-            send_block(vc, t, u, xrow(-d, h=1 - yh), sib, 0)
+        @pl.when(upper)
+        def _():
+            for d in (1, 3, 2):
+                arrived(vc, t, u, xrow(-d, h=1 - yh), 6 + d)
+                send_block(vc, t, u, xrow(-d, h=1 - yh), sib, 0)
+
+    def wait_blocks(buf, t, u, count, side, received):
+        some = blocks_of(buf, t, u, count)
+        cp = rcopy(some, some, ag_s.at[t, u, side], ag_r.at[t, u, 0], sib)
+        if received:
+            cp.wait_recv()
+        else:
+            cp.wait_send()
 
     def gathered(t, u):
-        eight = blocks_of(vc, t, u, 8)
-        rcopy(eight, eight, ag_s.at[t, u, 0], ag_r.at[t, u, 0], sib).wait_recv()
+        pl.when(upper)(lambda: wait_blocks(vc, t, u, 8, 0, True))
+        pl.when(lower)(lambda: wait_blocks(vc, t, u, 4, 0, True))
 
     def settle_gather(t, u):
-        sent = blocks_of(vc, t, u, 15)
-        rcopy(sent, sent, ag_s.at[t, u, 0], ag_r.at[t, u, 0], sib).wait_send()
-        sent = blocks_of(vr, t, u, 7)
-        rcopy(sent, sent, ag_s.at[t, u, 1], ag_r.at[t, u, 0], sib).wait_send()
+        pl.when(upper)(lambda: wait_blocks(vc, t, u, 14, 0, False))
+        pl.when(lower)(lambda: wait_blocks(vc, t, u, 8, 0, False))
+        wait_blocks(vr, t, u, 7, 1, False)
 
     centre = 0.5 * (top[...] + low[...])
     halfwidth = 0.5 * (top[...] - low[...])
@@ -295,12 +314,23 @@
         return rcopy(zs.at[t, u, 1, 2], zf.at[t, u], rs_s.at[t, u, 6], rs_r.at[t, u, 14], ylp)
 
     def settle_reduce(t, u):
-        rcopy(mx.at[t, u], mx.at[t, u], rs_s.at[t, u, 0], rs_r.at[t, u, 0], sib).wait_send()
-        rcopy(xr.at[t, u], xr.at[t, u], rs_s.at[t, u, 1], rs_r.at[t, u, 4], sib).wait_send()
+        def settle_x(own, got):
+            rcopy(own, own, rs_s.at[t, u, 0], rs_r.at[t, u, 0], sib).wait_send()
+            rcopy(got, got, rs_s.at[t, u, 1], rs_r.at[t, u, 4], sib).wait_send()
+
+        @pl.when(upper)
+        def _():
+            settle_x(mx.at[t, u], xr.at[t, u])
+            along_y(t, u)[0].wait_send()
+
+        @pl.when(lower)
+        def _():
+            settle_x(mx.at[t, u, 0], xr.at[t, u, 0])
+
         for e in range(2):
             sent = zr.at[t, u, e, pl.ds(0, 3 - e)]
             rcopy(sent, sent, rs_s.at[t, u, 2 + 3 * e], rs_r.at[t, u, 5], sib).wait_send()
-        for cp in along_y(t, u) + (far_z(t, u),):
+        for cp in (along_y(t, u)[1], far_z(t, u)):
             cp.wait_send()
 
     def products(t, u, e):
@@ -332,18 +362,29 @@
                 along_z(t, u, e, d).start()
 
         if e:
-            mirror(2)
-            mirror(1)
+            @pl.when(upper)
+            def _():
+                mirror(2)
+                mirror(1)
+
             pass_far(t, u)
-            mirror(3)
-            for d in (2, 1, 3):
-                mirror_on(d)
+
+            @pl.when(upper)
+            def _():
+                mirror(3)
+                for d in (2, 1, 3):
+                    mirror_on(d)
+
             gathered(t, u)
             for d in (2, 1, 3):
                 direct(d)
-            mirror(0)
+
+            @pl.when(upper)
+            def _():
+                mirror(0)
+                mirror_on(0)
+
             direct(0)
-            mirror_on(0)
         else:
             for d in (1, 3, 2):
                 mirror(d)
@@ -368,26 +409,27 @@
         rcopy(all_z, all_z, rs_s.at[t, u, 2], rs_r.at[t, u, 10 + e], sib).wait_recv()
 
     def reduce(t, u):
-        cp_y, cp_l = along_y(t, u)
-        arrived_x(t, u, 1)
-        ys[t, u] = summed(mx, xr, t, u, 1)
-        cp_y.start()
+        @pl.when(upper)
+        def _():
+            arrived_x(t, u, 1)
+            ys[t, u] = summed(mx, xr, t, u, 1)
+            along_y(t, u)[0].start()
+
         arrived_z(t, u, 1)
         ls[t, u] = (zs[t, u, 1, 0] + zr[t, u, 1, 0]) + zr[t, u, 1, 2]
-        cp_l.start()
+        along_y(t, u)[1].start()
 
     def update(t, u):
         span = slice(u * KH, (u + 1) * KH)
-        cp_y, cp_l = along_y(t, u)
         now = cur[span, :]
         own = product(now.astype(BF16), diag[...], 1, 1)
         arrived_x(t, u, 0)
         own += summed(mx, xr, t, u, 0)
         arrived_z(t, u, 0)
         own += summed(zs, zr, t, u, 0)
-        cp_y.wait_recv()
+        pl.when(lower)(lambda: along_y(t, u)[0].wait_recv())
         own += yr[t, u]
-        cp_l.wait_recv()
+        along_y(t, u)[1].wait_recv()
         own += lr[t, u]
         scale = jnp.where(t == 0, 1.0, 2.0).astype(F32)
         following = scale * (own - centre * now) / halfwidth - prev[span, :]
@@ -397,6 +439,10 @@
 
     for u in range(HALF):
         begin(0, u, cur[u * KH : (u + 1) * KH, :].astype(BF16))
+
+    @pl.when(lower)
+    def _():
+        vc[:, :, :, : NC * LR] = jnp.zeros((DEG + 1, HALF, KH, NC * LR), BF16)
 
     build_diag(onsite, diag)
     fetch.wait()

time: 129 us -> 126 us (0.977)
  Pallas kernels: 127 us -> 124 us
    pallas_call x1, Pallas kernels: 124 us -> 121 us  [local(): pl.pallas_call(kernel, out_shape=(rows, square, square), in_specs=[anywhe...]
where the time goes in v7:
time: 126 us
  Pallas kernels  124 us (98%)
  between operations  1.93 us (2%)
    pallas_call x1, Pallas kernels, local(): pl.pallas_call(kernel, out_shape=(rows, square, square), in_specs=[anywhe...  121 us
    pallas_call x1, Pallas kernels, local(): pl.pallas_call(project, out_shape=(rows, square), name='project')  2.9 us

profile of v7, /device:TPU:1, one launch (start us, length us, event | category | flops | bytes accessed | tf_op | source)
XLA Modules:
  0.0 126.1 jit_solution(12128075552748992157)
XLA Ops:
  1.9 121.3 %filter_and_project.1 = (f32[128,256]{1,0:T(8,128)}, f32[256,256]{1,0:T(8,128)}, f32[256,256]{1,0:T(8,128)}) custom-call(bf16[16,16,4096]{2,1,0:T(8,128)(2,1)} %hblocks.1, s32[16,16]{1,0:T(8,128)} %cols.1, s32[1,16]{1,0:T(1,128)} %bitcast.1, f32[128,256]{1,0:T(8,128)} %y0.1, bf16[2,4096]{1,0:T(2,128)(2,1)} %onsite.1, f32[1]{0:T(128)S(6)} %copy.9.low, ...), custom_call_target="tpu_custom_call" | custom-call | tf_op jit(solution)/shard_map/filter_and_project/pallas_call | solution.py:606
  123.2 2.9 %project.1 = (f32[128,256]{1,0:T(8,128)}, f32[256,256]{1,0:T(8,128)}) custom-call(f32[128,256]{1,0:T(8,128)} %get-tuple-element.5.made, f32[256,256]{1,0:T(8,128)} %get-tuple-element.6.inverse, f32[256,256]{1,0:T(8,128)} %get-tuple-element.7.half), custom_call_target="tpu_custom_call" | custom-call | tf_op jit(solution)/shard_map/project/pallas_call | solution.py:655

commit v8 on v7

--- a/solution.py
+++ b/solution.py
@@ -548,9 +548,9 @@
 
     rounded = cur[...].astype(BF16)
     part[0] = product(rounded, rounded, 1, 1)
-    to_row(0)
     for u in range(HALF):
         relay(DEG, u)
+    to_row(0)
     for u in range(HALF):
         pass_on(DEG, u)
         pass_far(DEG, u)

time: 126 us -> 126 us (level)
  no operation moved by 1% of the time
where the time goes in v8:
time: 126 us
  Pallas kernels  124 us (98%)
  between operations  1.93 us (2%)
    pallas_call x1, Pallas kernels, local(): pl.pallas_call(kernel, out_shape=(rows, square, square), in_specs=[anywhe...  121 us
    pallas_call x1, Pallas kernels, local(): pl.pallas_call(project, out_shape=(rows, square), name='project')  2.91 us

profile of v8, /device:TPU:1, one launch (start us, length us, event | category | flops | bytes accessed | tf_op | source)
XLA Modules:
  0.0 126.0 jit_solution(14089547268599346947)
XLA Ops:
  1.9 121.2 %filter_and_project.1 = (f32[128,256]{1,0:T(8,128)}, f32[256,256]{1,0:T(8,128)}, f32[256,256]{1,0:T(8,128)}) custom-call(bf16[16,16,4096]{2,1,0:T(8,128)(2,1)} %hblocks.1, s32[16,16]{1,0:T(8,128)} %cols.1, s32[1,16]{1,0:T(1,128)} %bitcast.1, f32[128,256]{1,0:T(8,128)} %y0.1, bf16[2,4096]{1,0:T(2,128)(2,1)} %onsite.1, f32[1]{0:T(128)S(6)} %copy.9.low, ...), custom_call_target="tpu_custom_call" | custom-call | tf_op jit(solution)/shard_map/filter_and_project/pallas_call | solution.py:606
  123.1 2.9 %project.1 = (f32[128,256]{1,0:T(8,128)}, f32[256,256]{1,0:T(8,128)}) custom-call(f32[128,256]{1,0:T(8,128)} %get-tuple-element.5.made, f32[256,256]{1,0:T(8,128)} %get-tuple-element.6.inverse, f32[256,256]{1,0:T(8,128)} %get-tuple-element.7.half), custom_call_target="tpu_custom_call" | custom-call | tf_op jit(solution)/shard_map/project/pallas_call | solution.py:655
